TPU v7x, 32 devices: a whole 2x2x4 slice. The times are simulated.
32 devices in a mesh: cons: 4 (over y, core), prod: 8 (over z, x).
Axes of the slice: x: 2, y: 2, z: 4, core: 2. Of those that a mesh axis runs over, the one named last changes fastest.
Arguments:
- tastes: bfloat16 [16384, 128], P('cons'), may hold values from -128 to 128
- price_coef: float32 [16384], P('cons'), may hold values from 0.5 to 5
- characteristics: bfloat16 [16384, 128], P('prod'), may hold values from -6 to 6
- mean_utility: float32 [16384], P('prod'), may hold values from -4 to 4
- panel_cols: int32 [256], replicated, may hold values from 0 to 16383
- firm_map: int32 [16384], P('prod'), may hold values from 0 to 16383, as said below
- inverses: float32 [128, 128, 128], P('prod'), may hold values from -0.5 to 0.5
Outputs:
- shares: float32 [16384], P('prod')
- markup: float32 [16384], P('prod')
- response: float32 [16384, 256], P('prod')
Inputs may be any that keep to these rules, and one draw needn't show every extreme that they name: `firm_map`: a permutation of the products; the rows of firm order held by each index of prod name exactly 256 products held by each index of prod.
All inputs are finite; a program needn't handle non-finite values.
Results may differ from a plain program's by a relative error of at most 0.002.
The roundings to bfloat16 on the way count: a program that leaves them out, or rounds other values in their place, can miss the bound.
Values may be sent and summed in bfloat16 or wider, within the bound.
A program may use at most 64 MiB of HBM per device.

v0:
```python
import jax
import jax.numpy as jnp
from jax import lax
from jax.sharding import PartitionSpec as P


def utilities(taste_block, characteristics, mean_utility):
    return (
        jnp.einsum("ik,jk->ij", taste_block, characteristics, preferred_element_type=jnp.float32)
        + mean_utility[None, :]
    )


def request_order(firm_map):
    local_count = firm_map.shape[0]
    holders = lax.axis_size("prod")
    per_pair = local_count // holders
    source = firm_map // local_count
    order = jnp.argsort(source, stable=True)
    wanted = firm_map[order].reshape(holders, per_pair)
    return (order, wanted)


def regroup(jacobian, shares, firm_map):
    local_count = jacobian.shape[0]
    order, wanted = request_order(firm_map)
    base = lax.axis_index("prod") * local_count
    local_ids = lax.all_to_all(wanted, "prod", split_axis=0, concat_axis=0, tiled=True) - base
    rows_out = jnp.take(jacobian, local_ids, axis=0)
    values_out = jnp.take(shares, local_ids, axis=0)
    rows_back = lax.all_to_all(rows_out, "prod", split_axis=0, concat_axis=0, tiled=True)
    values_back = lax.all_to_all(values_out, "prod", split_axis=0, concat_axis=0, tiled=True)
    flat_rows = rows_back.reshape(local_count, jacobian.shape[1])
    flat_values = values_back.reshape(local_count)
    placed_rows = jnp.zeros_like(flat_rows).at[order].set(flat_rows)
    placed_values = jnp.zeros_like(flat_values).at[order].set(flat_values)
    return (placed_rows, placed_values)


def apply_blocks(inverses, placed_rows, placed_values):
    firm_count, block_size = (inverses.shape[0], inverses.shape[1])
    ordered = placed_rows.reshape(firm_count, block_size, placed_rows.shape[1])
    response = jnp.einsum(
        "fab,fbc->fac", inverses, ordered, precision=lax.Precision.HIGHEST
    ).reshape(placed_rows.shape)
    markup = jnp.einsum(
        "fab,fb->fa",
        inverses,
        placed_values.reshape(firm_count, block_size),
        precision=lax.Precision.HIGHEST,
    ).reshape(placed_values.shape)
    return (response, markup)


def body(tastes, price_coef, characteristics, mean_utility, panel_cols, firm_map, inverses):
    local_products = characteristics.shape[0]
    local_consumers = tastes.shape[0]
    col_count = panel_cols.shape[0]
    count_products = local_products * lax.axis_size("prod")
    count_consumers = local_consumers * lax.axis_size("cons")
    product_ids = lax.axis_index("prod") * local_products + lax.iota(jnp.int32, local_products)
    hits = product_ids[None, :] == panel_cols[:, None]
    part_chars = jnp.dot(
        hits.astype(jnp.bfloat16), characteristics, preferred_element_type=jnp.float32
    )
    part_means = jnp.dot(hits.astype(jnp.float32), mean_utility, precision=lax.Precision.HIGHEST)
    col_chars, col_means = lax.psum((part_chars, part_means), "prod")
    used_chars, used_means, used_ids = (characteristics, mean_utility, product_ids)
    block_rows = min(512, local_consumers)
    block_count = local_consumers // block_rows
    taste_blocks = tastes.reshape(block_count, block_rows, tastes.shape[1])
    coef_blocks = price_coef.reshape(block_count, block_rows)

    def local_peak(taste_block):
        utility = utilities(taste_block, used_chars, used_means)
        return jnp.maximum(jnp.max(utility, axis=1), 0.0)

    highest = lax.pmax(lax.map(local_peak, taste_blocks).reshape(local_consumers), "prod")

    def local_sum(inputs):
        taste_block, peak_block = inputs
        utility = utilities(taste_block, used_chars, used_means)
        return jnp.sum(jnp.exp(utility - peak_block[:, None]), axis=1)

    partial_total = lax.map(local_sum, (taste_blocks, highest.reshape(block_count, block_rows)))
    total = lax.psum(partial_total.reshape(local_consumers), "prod")
    denominator = jnp.exp(-highest) + total

    def consume(state_now, inputs):
        panel_sum, share_sum, diag_sum = state_now
        taste_block, coef_block, peak_block, denom_block = inputs
        utility = utilities(taste_block, used_chars, used_means)
        scaled = count_products * jnp.exp(utility - peak_block[:, None]) / denom_block[:, None]
        share_sum = share_sum + jnp.sum(scaled, axis=0)
        diag_sum = diag_sum + jnp.dot(coef_block, scaled, precision=lax.Precision.HIGHEST)
        col_util = (
            jnp.dot(taste_block.astype(jnp.float32), col_chars.T, precision=lax.Precision.HIGHEST)
            + col_means[None, :]
        )
        col_scaled = count_products * jnp.exp(col_util - peak_block[:, None]) / denom_block[:, None]
        weighted = (coef_block[:, None] * col_scaled).astype(jnp.bfloat16)
        panel_sum = panel_sum + lax.dot_general(
            scaled.astype(jnp.bfloat16),
            weighted,
            (((0,), (0,)), ((), ())),
            preferred_element_type=jnp.float32,
        )
        return ((panel_sum, share_sum, diag_sum), None)

    start_state = (
        jnp.zeros((local_products, col_count), jnp.float32),
        jnp.zeros((local_products,), jnp.float32),
        jnp.zeros((local_products,), jnp.float32),
    )
    scan_inputs = (
        taste_blocks,
        coef_blocks,
        highest.reshape(block_count, block_rows),
        denominator.reshape(block_count, block_rows),
    )
    (panel_sum, share_sum, diag_sum), _ = lax.scan(consume, start_state, scan_inputs)
    marks = (used_ids[:, None] == panel_cols[None, :]).astype(jnp.float32)
    part_cols = col_count // lax.axis_size("cons")
    panel_part = lax.psum_scatter(panel_sum, "cons", scatter_dimension=1, tiled=True)
    share_all, diag_all = lax.psum((share_sum, diag_sum), "cons")
    mark_part = lax.dynamic_slice_in_dim(marks, lax.axis_index("cons") * part_cols, part_cols, 1)
    local_shares = share_all / count_consumers
    diagonal = diag_all / count_consumers
    jacobian = panel_part / count_consumers - diagonal[:, None] * mark_part
    placed_rows, placed_values = regroup(jacobian, local_shares, firm_map)
    response, markup = apply_blocks(inverses, placed_rows, placed_values)
    response = lax.all_gather(response, "cons", axis=1, tiled=True)
    return (local_shares, markup, response)


def solution(mesh):
    return jax.shard_map(
        body,
        mesh=mesh,
        in_specs=(
            P("cons", None),
            P("cons"),
            P("prod", None),
            P("prod"),
            P(),
            P("prod"),
            P("prod", None, None),
        ),
        out_specs=(P("prod"), P("prod"), P("prod", None)),
        check_vma=False,
    )
```

profile of v0, /device:TPU:0, one launch (start us, length us, event | category | flops | bytes accessed | tf_op | source)
XLA Modules:
  0.0 332.7 jit_solution(9404396025365228283)
XLA Ops:
  7.2 2.3 fusion.23
  9.6 15.6 %while.35 = (s32[]{:T(128)}, f32[8,512]{1,0:T(8,128)S(1)}, bf16[8,512,128]{2,1,0:T(8,128)(2,1)}, bf16[2048,128]{1,0:T(8,128)(2,1)}, f32[2048]{0:T(1024)}, /*index=5*/s32[]{:T(128)}, s32[]{:T(128)}) while((s32[]{:T(128)}, f32[8,512]{1,0:T(8,128)S(1)}, bf16[8,512,128]{2,1,0:T(8,128)(2,1)}, bf16[2048,128]{1,0:T(8,128)(2,1)}, f32[2048]{0:T(1024)}, ...), condition=%wide.region_2.3_spmd, body=%wide.region_0.2_spmd.sunk | while | flops 270532608 | bytes 674385 | solution.py:78
  13.5 1.9 add_reduce_fusion.2
  17.4 1.9 add_reduce_fusion.2
  19.4 1.9 add_reduce_fusion.2
  21.3 1.9 add_reduce_fusion.2
  25.3 38.9 %pmax.7 = f32[4096]{0:T(1024)S(1)} all-reduce(f32[4096]{0:T(1024)S(1)} %bitcast.120), channel_id=1, replica_groups=mesh['cons'=4,'prod'=8] {'prod'}, use_global_device_ids=true, to_apply=%region_3.0 | all-reduce | flops 4096 | bytes 32768 | tf_op jit(solution)/shard_map/pmax | solution.py:78
  64.1 16.9 %while.36 = (s32[]{:T(128)}, f32[8,512]{1,0:T(8,128)S(1)}, bf16[8,512,128]{2,1,0:T(8,128)(2,1)}, bf16[2048,128]{1,0:T(8,128)(2,1)}, f32[2048]{0:T(1024)}, /*index=5*/f32[8,512]{1,0:T(8,128)S(1)}, s32[]{:T(128)}, s32[]{:T(128)}) while((s32[]{:T(128)}, f32[8,512]{1,0:T(8,128)S(1)}, bf16[8,512,128]{2,1,0:T(8,128)(2,1)}, ...), condition=%wide.region_6.7_spmd, body=%wide.region_4.6_spmd.sunk | while | flops 271580672 | bytes 676445 | solution.py:85
  64.2 2.0 exponential_reduce_fusion.2
  66.3 2.0 exponential_reduce_fusion.2
  68.4 2.0 exponential_reduce_fusion.2
  70.5 2.0 exponential_reduce_fusion.2
  72.6 2.0 exponential_reduce_fusion.2
  74.7 2.0 exponential_reduce_fusion.2
  76.8 2.0 exponential_reduce_fusion.2
  79.0 2.0 exponential_reduce_fusion.2
  82.8 33.0 %all-reduce = (f32[4096]{0:T(1024)S(1)}, f32[256]{0:T(256)S(1)}) all-reduce(f32[4096]{0:T(1024)S(1)} %bitcast.119, f32[256]{0:T(256)S(1)} %bitcast.132), channel_id=1, replica_groups=mesh['cons'=4,'prod'=8] {'prod'}, use_global_device_ids=true, to_apply=%region_7.8 | all-reduce | flops 4352 | bytes 34816 | tf_op jit(solution)/shard_map/psum | solution.py:86
  115.9 93.8 %while.37 = (s32[]{:T(128)}, f32[2048,256]{1,0:T(8,128)S(1)}, f32[2048]{0:T(1024)S(1)}, f32[2048]{0:T(1024)S(1)}, bf16[8,512,128]{2,1,0:T(8,128)(2,1)}, /*index=...) while((s32[]{:T(128)}, f32[2048,256]{1,0:T(8,128)S(1)}, ...), condition=%wide.region_12.13_spmd.clone, body=%wide.region_10.12_spmd.clone.sunk | while | flops 1027348480 | bytes 35621072 | solution.py:121
  115.9 2.3 fusion.75
  118.3 1.9 copy-done.3
  120.1 2.1 fusion.76
  123.6 4.0 %convolution_add_fusion.3 = f32[2048,256]{1,0:T(8,128)S(1)} fusion(bf16[512,256]{1,0:T(8,128)(2,1)S(1)} %fusion.74, f32[2048,256]{1,0:T(8,128)S(1)} %get-tuple-element.451, f32[512,2048]{1,0:T(8,128)} %copy-done.3, pred[]{:T(512)S(6)} %compare.9), kind=kOutput, calls=%fused_computation.16.clone.1 | convolution fusion | flops 538968064 | bytes 8650753 | tf_op jit(solution)/shard_map/while/body/eval_jaxpr/dot_general | solution.py:102
  127.6 2.3 fusion.75
  130.0 1.9 copy-done.3
  131.9 2.1 fusion.76
  135.3 4.0 %convolution_add_fusion.3 = f32[2048,256]{1,0:T(8,128)S(1)} fusion(bf16[512,256]{1,0:T(8,128)(2,1)S(1)} %fusion.74, f32[2048,256]{1,0:T(8,128)S(1)} %get-tuple-element.451, f32[512,2048]{1,0:T(8,128)} %copy-done.3, pred[]{:T(512)S(6)} %compare.9), kind=kOutput, calls=%fused_computation.16.clone.1 | convolution fusion | flops 538968064 | bytes 8650753 | tf_op jit(solution)/shard_map/while/body/eval_jaxpr/dot_general | solution.py:102
  139.4 2.3 fusion.75
  141.7 1.9 copy-done.3
  143.6 2.1 fusion.76
  147.0 4.0 %convolution_add_fusion.3 = f32[2048,256]{1,0:T(8,128)S(1)} fusion(bf16[512,256]{1,0:T(8,128)(2,1)S(1)} %fusion.74, f32[2048,256]{1,0:T(8,128)S(1)} %get-tuple-element.451, f32[512,2048]{1,0:T(8,128)} %copy-done.3, pred[]{:T(512)S(6)} %compare.9), kind=kOutput, calls=%fused_computation.16.clone.1 | convolution fusion | flops 538968064 | bytes 8650753 | tf_op jit(solution)/shard_map/while/body/eval_jaxpr/dot_general | solution.py:102
  151.1 2.3 fusion.75
  153.4 1.9 copy-done.3
  155.3 2.1 fusion.76
  158.8 4.0 %convolution_add_fusion.3 = f32[2048,256]{1,0:T(8,128)S(1)} fusion(bf16[512,256]{1,0:T(8,128)(2,1)S(1)} %fusion.74, f32[2048,256]{1,0:T(8,128)S(1)} %get-tuple-element.451, f32[512,2048]{1,0:T(8,128)} %copy-done.3, pred[]{:T(512)S(6)} %compare.9), kind=kOutput, calls=%fused_computation.16.clone.1 | convolution fusion | flops 538968064 | bytes 8650753 | tf_op jit(solution)/shard_map/while/body/eval_jaxpr/dot_general | solution.py:102
  162.8 2.3 fusion.75
  165.1 1.9 copy-done.3
  167.0 2.1 fusion.76
  170.5 4.0 %convolution_add_fusion.3 = f32[2048,256]{1,0:T(8,128)S(1)} fusion(bf16[512,256]{1,0:T(8,128)(2,1)S(1)} %fusion.74, f32[2048,256]{1,0:T(8,128)S(1)} %get-tuple-element.451, f32[512,2048]{1,0:T(8,128)} %copy-done.3, pred[]{:T(512)S(6)} %compare.9), kind=kOutput, calls=%fused_computation.16.clone.1 | convolution fusion | flops 538968064 | bytes 8650753 | tf_op jit(solution)/shard_map/while/body/eval_jaxpr/dot_general | solution.py:102
  174.5 2.3 fusion.75
  176.9 1.9 copy-done.3
  178.7 2.1 fusion.76
  182.2 4.0 %convolution_add_fusion.3 = f32[2048,256]{1,0:T(8,128)S(1)} fusion(bf16[512,256]{1,0:T(8,128)(2,1)S(1)} %fusion.74, f32[2048,256]{1,0:T(8,128)S(1)} %get-tuple-element.451, f32[512,2048]{1,0:T(8,128)} %copy-done.3, pred[]{:T(512)S(6)} %compare.9), kind=kOutput, calls=%fused_computation.16.clone.1 | convolution fusion | flops 538968064 | bytes 8650753 | tf_op jit(solution)/shard_map/while/body/eval_jaxpr/dot_general | solution.py:102
  186.3 2.3 fusion.75
  188.6 1.9 copy-done.3
  190.5 2.1 fusion.76
  193.9 4.0 %convolution_add_fusion.3 = f32[2048,256]{1,0:T(8,128)S(1)} fusion(bf16[512,256]{1,0:T(8,128)(2,1)S(1)} %fusion.74, f32[2048,256]{1,0:T(8,128)S(1)} %get-tuple-element.451, f32[512,2048]{1,0:T(8,128)} %copy-done.3, pred[]{:T(512)S(6)} %compare.9), kind=kOutput, calls=%fused_computation.16.clone.1 | convolution fusion | flops 538968064 | bytes 8650753 | tf_op jit(solution)/shard_map/while/body/eval_jaxpr/dot_general | solution.py:102
  198.0 2.3 fusion.75
  200.3 1.9 copy-done.3
  202.2 2.1 fusion.76
  205.6 4.0 %convolution_add_fusion.3 = f32[2048,256]{1,0:T(8,128)S(1)} fusion(bf16[512,256]{1,0:T(8,128)(2,1)S(1)} %fusion.74, f32[2048,256]{1,0:T(8,128)S(1)} %get-tuple-element.451, f32[512,2048]{1,0:T(8,128)} %copy-done.3, pred[]{:T(512)S(6)} %compare.9), kind=kOutput, calls=%fused_computation.16.clone.1 | convolution fusion | flops 538968064 | bytes 8650753 | tf_op jit(solution)/shard_map/while/body/eval_jaxpr/dot_general | solution.py:102
  211.5 5.0 %sort.17 = (s32[2048]{0:T(1024)}, s32[2048]{0:T(1024)S(1)}) sort(s32[2048]{0:T(1024)S(1)} %add_select_fusion, s32[2048]{0:T(1024)S(1)} %iota.12), dimensions={0}, to_apply=%region_14.15 | sort | flops 22528 | bytes 32768 | tf_op jit(solution)/shard_map/jit(argsort)/sort | solution.py:19
  216.6 20.5 %gather_fusion = s32[2048]{0:T(1024)} fusion(s32[2048]{0:T(1024)S(1)} %copy-done.1, s32[2048]{0:T(1024)S(1)} %get-tuple-element.240), kind=kCustom, calls=%fused_computation | custom fusion | bytes 24576 | tf_op jit(solution)/shard_map/gather | solution.py:20
  237.1 3.3 %all-to-all-start = ((s32[8,1,256]{2,1,0:T(1,128)}), s32[8,1,256]{2,1,0:T(1,128)S(1)}, u32[]{:S(2)}, u32[]{:S(2)}) async-start(s32[8,1,256]{2,1,0:T(1,128)} %bitcast.8), calls=%async_computation | async-start | bytes 16384 | tf_op jit(solution)/shard_map/all_to_all | solution.py:28
  240.6 6.3 %all-to-all-done = s32[8,1,256]{2,1,0:T(1,128)S(1)} async-done(((s32[8,1,256]{2,1,0:T(1,128)}), s32[8,1,256]{2,1,0:T(1,128)S(1)}, u32[]{:S(2)}, u32[]{:S(2)}) %all-to-all-start) | async-done | bytes 8224 | tf_op jit(solution)/shard_map/all_to_all | solution.py:28
  247.0 10.3 %all-reduce.1 = (f32[2048]{0:T(1024)S(1)}, f32[2048]{0:T(1024)S(1)}) all-reduce(f32[2048]{0:T(1024)S(1)} %get-tuple-element.129, f32[2048]{0:T(1024)S(1)} %get-tuple-element.132), channel_id=1, replica_groups=mesh['cons'=4,'prod'=8] {'cons'}, use_global_device_ids=true, to_apply=%region_13.14 | all-reduce | flops 4096 | bytes 32768 | tf_op jit(solution)/shard_map/psum | solution.py:125
  259.4 5.5 %gather_fusion.2 = f32[2048,64]{1,0:T(8,128)S(1)} fusion(f32[2048,64]{1,0:T(8,128)S(1)} %multiply_subtract_fusion, s32[2048]{0:T(1024)S(1)} %broadcast_clamp_fusion), kind=kCustom, calls=%fused_computation.2 | custom fusion | bytes 1056768 | tf_op jit(solution)/shard_map/jit(_take)/gather | solution.py:29
  265.3 16.7 %all_to_all.20 = f32[8,256,64]{1,2,0:T(8,128)S(1)} all-to-all(f32[8,256,64]{1,2,0:T(8,128)S(1)} %broadcast_select_fusion), channel_id=1, replica_groups=mesh['cons'=4,'prod'=8] {'prod'}, dimensions={0} | all-to-all | bytes 1048576 | tf_op jit(solution)/shard_map/all_to_all | solution.py:31
  282.3 5.8 %scatter_custom_fusion.1 = f32[2048,64]{1,0:T(8,128)S(1)} fusion(s32[2048]{0:T(1024)S(1)} %get-tuple-element.241, f32[2048,64]{1,0:T(8,128)S(1)} %bitcast.112, f32[]{:T(128)} %constant.94.clone.1), kind=kCustom, calls=%fused_computation.49 | custom fusion | bytes 524292 | tf_op jit(solution)/shard_map/scatter | solution.py:35
  288.1 2.0 convolution_bitcast_fusion
  291.1 11.8 %gather_fusion.1 = f32[2048]{0:T(1024)S(1)} fusion(f32[2048]{0:T(1024)S(1)} %broadcast_multiply_fusion.1, s32[2048]{0:T(1024)S(1)} %broadcast_clamp_fusion), kind=kCustom, calls=%fused_computation.1 | custom fusion | bytes 24576 | tf_op jit(solution)/shard_map/jit(_take)/gather | solution.py:30
  302.9 9.9 %all_to_all.21 = f32[8,1,256]{2,1,0:T(1,128)S(1)} all-to-all(f32[8,1,256]{2,1,0:T(1,128)S(1)} %and_select_fusion), channel_id=1, replica_groups=mesh['cons'=4,'prod'=8] {'prod'}, dimensions={0} | all-to-all | bytes 16384 | tf_op jit(solution)/shard_map/all_to_all | solution.py:32
  312.8 8.0 %scatter_custom_fusion = f32[2048]{0:T(1024)S(1)} fusion(s32[2048]{0:T(1024)S(1)} %get-tuple-element.241, f32[2048]{0:T(1024)S(1)} %bitcast.131, f32[]{:T(128)} %constant.94.clone.1), kind=kCustom, calls=%fused_computation.72 | custom fusion | bytes 8196 | tf_op jit(solution)/shard_map/scatter | solution.py:36
  320.9 2.3 fusion.36
  323.3 2.9 copy.29
  (149 shorter events, 27.3 us)
Async XLA Ops:
  7.2 281.0 %copy-start = (f32[16,128,128]{2,1,0:T(8,128)S(1)}, f32[16,128,128]{2,1,0:T(8,128)}, u32[]{:S(2)}) copy-start(f32[16,128,128]{2,1,0:T(8,128)} %param.19) | copy-start | bytes 3145732
  7.2 108.7 %all-reduce.4.cloned.1.call-start = ((), (), s32[]{:S(2)}) async-start(), calls=%async_computation.4 | async-start | bytes 262144 | tf_op jit(solution)/shard_map/psum | solution.py:67
  9.5 247.8 %reduce-scatter.4.cloned.1.call-start = ((), (), s32[]{:S(2)}) async-start(), calls=%async_computation.6 | async-start | bytes 2621440
  64.1 16.9 %copy-start.6 = (s32[256]{0:T(256)S(1)}, s32[256]{0:T(256)}, u32[]{:S(2)}) copy-start(s32[256]{0:T(256)} %param.17) | copy-start | bytes 3076
  64.1 51.7 %copy-start.4 = (f32[4096]{0:T(1024)S(1)}, f32[4096]{0:T(1024)}, u32[]{:S(2)}) copy-start(f32[4096]{0:T(1024)} %param.14) | copy-start | bytes 49156
  118.2 1.9 copy-start.3
  118.2 4.0 %copy-start.5 = (f32[256,128]{1,0:T(8,128)S(1)}, f32[256,128]{1,0:T(8,128)}, u32[]{:S(2)}) copy-start(f32[256,128]{1,0:T(8,128)} %get-tuple-element.474) | copy-start | bytes 393220 | tf_op jit(solution)/shard_map/while
  129.9 1.9 copy-start.3
  129.9 4.0 %copy-start.5 = (f32[256,128]{1,0:T(8,128)S(1)}, f32[256,128]{1,0:T(8,128)}, u32[]{:S(2)}) copy-start(f32[256,128]{1,0:T(8,128)} %get-tuple-element.474) | copy-start | bytes 393220 | tf_op jit(solution)/shard_map/while
  141.7 1.9 copy-start.3
  141.7 4.0 %copy-start.5 = (f32[256,128]{1,0:T(8,128)S(1)}, f32[256,128]{1,0:T(8,128)}, u32[]{:S(2)}) copy-start(f32[256,128]{1,0:T(8,128)} %get-tuple-element.474) | copy-start | bytes 393220 | tf_op jit(solution)/shard_map/while
  153.4 1.9 copy-start.3
  153.4 4.0 %copy-start.5 = (f32[256,128]{1,0:T(8,128)S(1)}, f32[256,128]{1,0:T(8,128)}, u32[]{:S(2)}) copy-start(f32[256,128]{1,0:T(8,128)} %get-tuple-element.474) | copy-start | bytes 393220 | tf_op jit(solution)/shard_map/while
  165.1 1.9 copy-start.3
  165.1 4.0 %copy-start.5 = (f32[256,128]{1,0:T(8,128)S(1)}, f32[256,128]{1,0:T(8,128)}, u32[]{:S(2)}) copy-start(f32[256,128]{1,0:T(8,128)} %get-tuple-element.474) | copy-start | bytes 393220 | tf_op jit(solution)/shard_map/while
  176.8 1.9 copy-start.3
  176.8 4.0 %copy-start.5 = (f32[256,128]{1,0:T(8,128)S(1)}, f32[256,128]{1,0:T(8,128)}, u32[]{:S(2)}) copy-start(f32[256,128]{1,0:T(8,128)} %get-tuple-element.474) | copy-start | bytes 393220 | tf_op jit(solution)/shard_map/while
  188.5 1.9 copy-start.3
  188.6 4.0 %copy-start.5 = (f32[256,128]{1,0:T(8,128)S(1)}, f32[256,128]{1,0:T(8,128)}, u32[]{:S(2)}) copy-start(f32[256,128]{1,0:T(8,128)} %get-tuple-element.474) | copy-start | bytes 393220 | tf_op jit(solution)/shard_map/while
  200.3 1.9 copy-start.3
  200.3 4.0 %copy-start.5 = (f32[256,128]{1,0:T(8,128)S(1)}, f32[256,128]{1,0:T(8,128)}, u32[]{:S(2)}) copy-start(f32[256,128]{1,0:T(8,128)} %get-tuple-element.474) | copy-start | bytes 393220 | tf_op jit(solution)/shard_map/while
  209.7 1.9 copy-start.1
  237.1 9.8 %all-to-all-start = ((s32[8,1,256]{2,1,0:T(1,128)}), s32[8,1,256]{2,1,0:T(1,128)S(1)}, u32[]{:S(2)}, u32[]{:S(2)}) async-start(s32[8,1,256]{2,1,0:T(1,128)} %bitcast.8), calls=%async_computation | async-start | bytes 16384 | tf_op jit(solution)/shard_map/all_to_all | solution.py:28
  240.5 82.8 %all-gather.2.cloned.1.call-start = ((), (), s32[]{:S(2)}) async-start(), calls=%async_computation.5 | async-start | bytes 2621440 | tf_op jit(solution)/shard_map/all_gather | solution.py:132
  291.1 11.8 %copy-start.2 = (f32[2048]{0:T(1024)}, f32[2048]{0:T(1024)S(1)}, u32[]{:S(2)}) copy-start(f32[2048]{0:T(1024)S(1)} %broadcast_multiply_fusion.1) | copy-start | bytes 24580
Sparse Core Ops, SparseCore 0:
  11.9 73.2 all-reduce.3
  211.6 28.5 reduce-scatter.3
  291.2 20.6 all-gather.1
where the time goes:
time: 334 us; the launch traced here: 333 us
  matrix products  117 us (35%)
  blocking collectives  109 us (33%)
  local copies, waits for them, and re-layouts  75.8 us (23%)
  between operations  14.1 us (4%)
  waiting for transfers between devices  6.41 us (2%)
  other arithmetic  6 us (2%)
  starting transfers between devices  3.46 us (1%)
    dot_general x24, matrix products, utilities(): jnp.einsum('ik,jk->ij', taste_block, characteristics, preferred_element_t...  49.2 us
    pmax x1, blocking collectives, body(): lax.pmax(lax.map(local_peak, taste_blocks).reshape(local_consumers), 'prod')  38.9 us
    psum x1, blocking collectives, body(): total = lax.psum(partial_total.reshape(local_consumers), 'prod')  33 us
    dot_general x8, matrix products, consume(): lax.dot_general(scaled.astype(jnp.bfloat16), weighted, (((0,), (0,)), (()...  32 us
    gather x1, local copies, waits for them, and re-layouts, request_order(): wanted = firm_map[order].reshape(holders, per_pair)  20.5 us
    all_to_all x1, blocking collectives, regroup(): lax.all_to_all(rows_out, 'prod', split_axis=0, concat_axis=0, tiled=True)  16.7 us
    dot_general x8, matrix products, consume(): jnp.dot(coef_block, scaled, precision=lax.Precision.HIGHEST)  16.6 us
    while x32, local copies, waits for them, and re-layouts  15.2 us
  transfers between devices with their start and end apart: 4, of which 1 were waited for; matrix products, arithmetic and copies ran while one was open for 25% of the time, Pallas kernels for 0%

commit v1 on v0

v1 whole, which is shorter than its diff:
```python
import functools
import jax
import jax.numpy as jnp
from jax import lax
from jax.experimental import pallas as pl
from jax.experimental.pallas import tpu as pltpu
from jax.sharding import PartitionSpec as P

F32 = jnp.float32
BF16 = jnp.bfloat16
NT = (((1,), (1,)), ((), ()))
MESH = pl.DeviceIdType.MESH
VMEM = pl.BlockSpec(memory_space=pltpu.VMEM)
LIMIT = 63 * 1024 * 1024


def exchange_kernel(n, x_ref, o_ref, ssem, rsem, lsem):
    me = lax.axis_index("prod")
    barrier = pltpu.get_barrier_semaphore()
    for d in range(1, n):
        pl.semaphore_signal(barrier, inc=1, device_id={"prod": lax.rem(me + d, n)}, device_id_type=MESH)
    pl.semaphore_wait(barrier, n - 1)
    copies = []
    for d in range(1, n):
        peer = lax.rem(me + d, n)
        copy = pltpu.make_async_remote_copy(
            x_ref.at[peer], o_ref.at[me], ssem.at[d], rsem.at[d],
            device_id={"prod": peer}, device_id_type=MESH,
        )
        copy.start()
        copies.append(copy)
    own = pltpu.make_async_copy(x_ref.at[me], o_ref.at[me], lsem)
    own.start()
    own.wait()
    for copy in copies:
        copy.wait()


def exchange(x, cid):
    n = x.shape[0]
    return pl.pallas_call(
        functools.partial(exchange_kernel, n),
        out_shape=jax.ShapeDtypeStruct(x.shape, x.dtype),
        in_specs=[VMEM],
        out_specs=VMEM,
        scratch_shapes=[
            pltpu.SemaphoreType.DMA((n,)),
            pltpu.SemaphoreType.DMA((n,)),
            pltpu.SemaphoreType.DMA(()),
        ],
        compiler_params=pltpu.CompilerParams(collective_id=cid, has_side_effects=True),
    )(x)


def main_kernel(
    n, count_products, count_consumers, IC, JT,
    C, T, coef, colpart, inv, ids, cols,
    out, sm,
    E, MS, CC, FL, WT, PO, PX, PR, YS, YR, ST,
    ms_s, ms_r, cc_s, cc_r, px_s, px_r, y_s, y_r, st_s, st_r, o_s, o_r,
):
    me = lax.axis_index("prod")
    cons = lax.axis_index("cons")
    core = lax.rem(cons, 2)
    partner = cons + 1 - 2 * core
    across = lax.rem(cons + 2, 4)
    LP = C.shape[0]
    LI = T.shape[0]
    nc, nt = LI // IC, LP // JT
    half = out.shape[1] // 2
    block = inv.shape[1]

    barrier = pltpu.get_barrier_semaphore()
    for d in range(1, n):
        pl.semaphore_signal(barrier, inc=1, device_id={"prod": lax.rem(me + d, n)}, device_id_type=MESH)
    for d in range(1, 4):
        pl.semaphore_signal(barrier, inc=1, device_id={"cons": lax.rem(cons + d, 4)}, device_id_type=MESH)
    pl.semaphore_wait(barrier, n + 2)

    def cc_copy(d):
        return pltpu.make_async_remote_copy(
            colpart, CC.at[me], cc_s.at[d], cc_r.at[d],
            device_id={"prod": lax.rem(me + d, n)}, device_id_type=MESH,
        )

    def ms_copy(d, ic):
        return pltpu.make_async_remote_copy(
            MS.at[0, ic], MS.at[d, ic], ms_s.at[d, ic], ms_r.at[d, ic],
            device_id={"prod": lax.rem(me + d, n)}, device_id_type=MESH,
        )

    def each_peer(fn):
        def step(d, carry):
            fn(d)
            return carry
        lax.fori_loop(1, n, step, 0)

    each_peer(lambda d: cc_copy(d).start())
    CC[me] = colpart[...]

    def pass_one(ic, carry):
        i0 = pl.multiple_of(ic * IC, IC)
        tb = T[pl.ds(i0, IC), :]

        def utility(jt, m8):
            rows = pl.ds(pl.multiple_of(jt * JT, JT), JT)
            u = lax.dot_general(C[rows, :], tb, NT, preferred_element_type=F32)
            E[rows, pl.ds(i0, IC)] = u
            return jnp.maximum(m8, jnp.max(u.reshape(JT // 8, 8, IC), axis=0))

        m8 = lax.fori_loop(0, nt, utility, jnp.zeros((8, IC), F32))
        m = jnp.max(m8, axis=0, keepdims=True)

        def expo(jt, s8):
            rows = pl.ds(pl.multiple_of(jt * JT, JT), JT)
            e = jnp.exp(E[rows, pl.ds(i0, IC)] - m)
            E[rows, pl.ds(i0, IC)] = e
            return s8 + jnp.sum(e.reshape(JT // 8, 8, IC), axis=0)

        s8 = lax.fori_loop(0, nt, expo, jnp.zeros((8, IC), F32))
        MS[0, ic, 0:1, :] = m
        MS[0, ic, 1:2, :] = jnp.sum(s8, axis=0, keepdims=True)
        each_peer(lambda d: ms_copy(d, ic).start())
        return carry

    lax.fori_loop(0, nc, pass_one, 0)
    each_peer(lambda d: cc_copy(d).wait())
    ccv = CC[...].reshape(CC.shape[0] * CC.shape[1], CC.shape[2]).astype(BF16)

    def weights(ic, carry):
        each_peer(lambda d: ms_copy(d, ic).wait())
        i0 = pl.multiple_of(ic * IC, IC)
        peak = MS[0, ic, 0:1, :]
        for d in range(1, n):
            peak = jnp.maximum(peak, MS[d, ic, 0:1, :])
        den = jnp.exp(-peak)
        for d in range(n):
            den = den + MS[d, ic, 1:2, :] * jnp.exp(MS[d, ic, 0:1, :] - peak)
        f = count_products / den
        FL[:, pl.ds(i0, IC)] = jnp.exp(MS[0, ic, 0:1, :] - peak) * f
        cu = lax.dot_general(ccv, T[pl.ds(i0, IC), :], NT, preferred_element_type=F32)
        w = coef[:, pl.ds(i0, IC)] * (f * jnp.exp(cu - peak))
        WT[pl.ds(i0, IC), :] = w.T.astype(BF16)
        return carry

    lax.fori_loop(0, nc, weights, 0)

    def px_copy(jt):
        rows = pl.ds(pl.multiple_of(jt * JT, JT), JT)
        return pltpu.make_async_remote_copy(
            PX.at[rows], PR.at[rows], px_s.at[jt], px_r.at[jt],
            device_id={"cons": partner}, device_id_type=MESH,
        )

    def y_copy(jt):
        rows = pl.ds(pl.multiple_of(jt * JT, JT), JT)
        return pltpu.make_async_remote_copy(
            YS.at[rows], YR.at[rows], y_s.at[jt], y_r.at[jt],
            device_id={"cons": across}, device_id_type=MESH,
        )

    def o_copy(jt):
        rows = pl.ds(pl.multiple_of(jt * JT, JT), JT)
        mine = pl.ds(pl.multiple_of(core * half, half), half)
        return pltpu.make_async_remote_copy(
            out.at[rows, mine], out.at[rows, mine], o_s.at[jt], o_r.at[jt],
            device_id={"cons": partner}, device_id_type=MESH,
        )

    def st_copy(d):
        return pltpu.make_async_remote_copy(
            ST.at[cons], ST.at[cons], st_s.at[d], st_r.at[d],
            device_id={"cons": lax.rem(cons + d, 4)}, device_id_type=MESH,
        )

    def forward(jt):
        rows = pl.ds(pl.multiple_of(jt * JT, JT), JT)
        px_copy(jt).wait()
        YS[rows, :] = (PO[rows, :] + PR[rows, :]).astype(BF16)
        y_copy(jt).start()

    def panel(jt, carry):
        rows = pl.ds(pl.multiple_of(jt * JT, JT), JT)

        def over(ic, state):
            acc, sh, dg = state
            i0 = pl.multiple_of(ic * IC, IC)
            sc = E[rows, pl.ds(i0, IC)] * FL[:, pl.ds(i0, IC)]
            acc = acc + jnp.dot(sc.astype(BF16), WT[pl.ds(i0, IC), :], preferred_element_type=F32)
            cs = sc * coef[:, pl.ds(i0, IC)]
            for b in range(IC // 128):
                sh = sh + sc[:, b * 128:(b + 1) * 128]
                dg = dg + cs[:, b * 128:(b + 1) * 128]
            return acc, sh, dg

        zero = jnp.zeros((JT, 128), F32)
        acc, sh, dg = lax.fori_loop(0, nc, over, (jnp.zeros((JT, 2 * half), F32), zero, zero))
        first, second = acc[:, :half], acc[:, half:]
        PO[rows, :] = jnp.where(core == 0, first, second)
        PX[rows, :] = jnp.where(core == 0, second, first)
        px_copy(jt).start()
        ST[cons, 0:1, rows] = jnp.sum(sh.T, axis=0, keepdims=True)
        ST[cons, 1:2, rows] = jnp.sum(dg.T, axis=0, keepdims=True)

        @pl.when(jt > 0)
        def _():
            forward(jt - 1)

        return carry

    lax.fori_loop(0, nt, panel, 0)
    for d in range(1, 4):
        st_copy(d).start()
    forward(nt - 1)
    for d in range(1, 4):
        st_copy(d).wait()
    sm[0:1, :] = (ST[0, 0:1, :] + ST[1, 0:1, :] + ST[2, 0:1, :] + ST[3, 0:1, :]) / count_consumers
    ST[0, 1:2, :] = (ST[0, 1:2, :] + ST[1, 1:2, :] + ST[2, 1:2, :] + ST[3, 1:2, :]) / count_consumers
    mine = pl.ds(pl.multiple_of(core * half, half), half)
    heads = cols[:, mine]

    def finish(jt, carry):
        y_copy(jt).wait()
        for b in range(JT // block):
            r0 = pl.multiple_of(jt * JT + b * block, block)
            rows = pl.ds(r0, block)
            fb = jt * (JT // block) + b
            x = (YS[rows, :].astype(F32) + YR[rows, :].astype(F32)) / count_consumers
            diag = jnp.broadcast_to(ST[0, 1:2, rows], (half, block)).T
            jac = x - jnp.where(ids[rows, :] == heads, diag, 0.0)
            m = inv[fb]
            out[rows, mine] = jnp.dot(m, jac, precision=lax.Precision.HIGHEST, preferred_element_type=F32)
            share8 = jnp.broadcast_to(sm[0:1, rows], (8, block))
            mk = lax.dot_general(share8, m, NT, precision=lax.Precision.HIGHEST, preferred_element_type=F32)
            sm[1:2, rows] = mk[0:1, :]
        o_copy(jt).start()
        return carry

    lax.fori_loop(0, nt, finish, 0)

    def drain(jt, carry):
        o_copy(jt).wait()
        return carry

    lax.fori_loop(0, nt, drain, 0)


def run_main(n, caug, taug, coef, colpart, inverses, ids, cols, count_products, count_consumers):
    LP, LI, W = caug.shape[0], taug.shape[0], cols.shape[1]
    KA = caug.shape[1]
    IC, JT = min(512, LI), min(256, LP)
    nc, nt = LI // IC, LP // JT
    half = W // 2
    dma = pltpu.SemaphoreType.DMA
    return pl.pallas_call(
        functools.partial(main_kernel, n, float(count_products), float(count_consumers), IC, JT),
        out_shape=(jax.ShapeDtypeStruct((LP, W), F32), jax.ShapeDtypeStruct((2, LP), F32)),
        in_specs=[VMEM] * 7,
        out_specs=(VMEM, VMEM),
        scratch_shapes=[
            pltpu.VMEM((LP, LI), F32),
            pltpu.VMEM((n, nc, 2, IC), F32),
            pltpu.VMEM((n, W // n, KA), F32),
            pltpu.VMEM((1, LI), F32),
            pltpu.VMEM((LI, W), BF16),
            pltpu.VMEM((LP, half), F32),
            pltpu.VMEM((LP, half), F32),
            pltpu.VMEM((LP, half), F32),
            pltpu.VMEM((LP, half), BF16),
            pltpu.VMEM((LP, half), BF16),
            pltpu.VMEM((4, 2, LP), F32),
            dma((n, nc)), dma((n, nc)), dma((n,)), dma((n,)),
            dma((nt,)), dma((nt,)), dma((nt,)), dma((nt,)),
            dma((4,)), dma((4,)), dma((nt,)), dma((nt,)),
        ],
        compiler_params=pltpu.CompilerParams(
            collective_id=7, has_side_effects=True, vmem_limit_bytes=LIMIT
        ),
    )(caug, taug, coef, colpart, inverses, ids, cols)


def split_mean(mean):
    a = lax.reduce_precision(mean, 8, 7)
    b = lax.reduce_precision(mean - a, 8, 7)
    c = mean - a - b
    return jnp.stack([a.astype(BF16), b.astype(BF16), c.astype(BF16)], axis=1)


def lanes(count):
    return -(-count // 128) * 128


def body(tastes, price_coef, characteristics, mean_utility, panel_cols, firm_map, inverses):
    n = lax.axis_size("prod")
    LP, K = characteristics.shape
    LI = tastes.shape[0]
    W = panel_cols.shape[0]
    count_products = LP * n
    count_consumers = LI * lax.axis_size("cons")
    pp, cp = LP // n, W // n
    KA = 2 * K
    base = lax.axis_index("prod") * LP
    local = lax.iota(jnp.int32, LP)

    sid = lax.sort(firm_map)
    wanted = jnp.pad(sid.reshape(n, 1, pp), ((0, 0), (0, 0), (0, lanes(pp) - pp)))
    asked = exchange(wanted, 1)[:, 0, :pp].reshape(LP) - base

    caug = jnp.concatenate(
        [characteristics, split_mean(mean_utility), jnp.zeros((LP, KA - K - 3), BF16)], axis=1
    )
    picks = jnp.concatenate([asked, panel_cols - base])
    hot = (picks[:, None] == local[None, :]).astype(BF16)
    got = jnp.dot(hot, caug, preferred_element_type=F32).astype(BF16)
    mine = jnp.concatenate([got[:LP].reshape(n, pp, KA), got[LP:].reshape(n, cp, KA)], axis=1)
    each = pp + cp
    wide = lanes(each)
    means = jnp.pad(mine[:, :, K:K + 3].transpose(0, 2, 1), ((0, 0), (0, 0), (0, wide - each)))
    means = means.reshape(n, 3 * wide // 128, 128)
    total = each + means.shape[1]
    fill = -(-total // 16) * 16 - total
    sent = jnp.concatenate([mine[:, :, :K], means, jnp.zeros((n, fill, K), BF16)], axis=1)
    back = exchange(sent, 2)
    means_back = back[:, each:total].reshape(n, 3, wide)[:, :, :each].transpose(0, 2, 1)
    both = jnp.concatenate([back[:, :each], means_back, jnp.zeros((n, each, KA - K - 3), BF16)], axis=2)
    colpart = jnp.sum(both[:, pp:].astype(F32), axis=0)
    turn = (firm_map[:, None] == sid[None, :]).astype(BF16)
    cfirm = jnp.dot(turn, both[:, :pp].reshape(LP, KA), preferred_element_type=F32).astype(BF16)
    taug = jnp.concatenate(
        [tastes, jnp.ones((LI, 3), BF16), jnp.zeros((LI, KA - K - 3), BF16)], axis=1
    )
    response, sm = run_main(
        n, cfirm, taug, price_coef[None, :], colpart, inverses,
        firm_map[:, None], panel_cols[None, :], count_products, count_consumers,
    )
    values = jnp.sum(jnp.where(firm_map[:, None] == sid[None, :], sm[0][:, None], 0.0), axis=0)
    values = jnp.pad(values.reshape(n, 1, pp), ((0, 0), (0, 0), (0, lanes(pp) - pp)))
    home = exchange(values, 3)[:, 0, :pp].reshape(LP)
    shares = jnp.sum(jnp.where(asked[:, None] == local[None, :], home[:, None], 0.0), axis=0)
    return shares, sm[1], response


def solution(mesh):
    return jax.shard_map(
        body,
        mesh=mesh,
        in_specs=(
            P("cons", None),
            P("cons"),
            P("prod", None),
            P("prod"),
            P(),
            P("prod"),
            P("prod", None, None),
        ),
        out_specs=(P("prod"), P("prod"), P("prod", None)),
        check_vma=False,
    )
```

time: 334 us -> 140 us (0.42)
  matrix products: 117 us -> 7.2 us
  blocking collectives: 109 us -> 0 us
  Pallas kernels: 0 us -> 102 us
  local copies, waits for them, and re-layouts: 75.8 us -> 11.3 us
  between operations: 14.1 us -> 0.83 us
  other arithmetic: 6 us -> 18.2 us
  waiting for transfers between devices: 6.41 us -> 0 us
  starting transfers between devices: 3.46 us -> 0 us
    dot_general x52 -> x2, matrix products: 117 us -> 7.2 us  [the longest x1 3.68 us: body(): got = jnp.dot(hot, caug, preferred_element_type=F32).astype(BF16)]
    pallas_call x0 -> x4, Pallas kernels: none -> 102 us  [the longest x1 69.4 us: run_main(): pl.pallas_call(functools.partial(main_kernel, n, float(count_products), f...]
    psum x2 -> x0, blocking collectives: 43.4 us -> none  [the longest x1 33 us: body(): total = lax.psum(partial_total.reshape(local_consumers), 'prod')]
    pmax x1 -> x0, blocking collectives: 38.9 us -> none  [body(): lax.pmax(lax.map(local_peak, taste_blocks).reshape(local_consumers), 'prod')]
    gather x4 -> x0, local copies, waits for them, and re-layouts: 38.1 us -> none  [the longest x1 20.5 us: request_order(): wanted = firm_map[order].reshape(holders, per_pair)]
    all_to_all x2 -> x0, blocking collectives: 26.6 us -> none  [the longest x1 16.7 us: regroup(): lax.all_to_all(rows_out, 'prod', split_axis=0, concat_axis=0, tiled=True)]
    while x32 -> x0, local copies, waits for them, and re-layouts: 15.2 us -> none
    scatter x2 -> x0, local copies, waits for them, and re-layouts: 13.9 us -> none  [the longest x1 8.05 us: regroup(): placed_values = jnp.zeros_like(flat_values).at[order].set(flat_values)]
  transfers between devices with their start and end apart: 4 -> 0, of which waited for: 1 -> 0; matrix products, arithmetic and copies ran while one was open for 25% -> 0% of each run, Pallas kernels for 0% -> 0%
where the time goes in v1:
time: 140 us; the launch traced here: 139 us
  Pallas kernels  102 us (73%)
  other arithmetic  18.2 us (13%)
  local copies, waits for them, and re-layouts  11.3 us (8%)
  matrix products  7.2 us (5%)
    pallas_call x1, Pallas kernels, run_main(): pl.pallas_call(functools.partial(main_kernel, n, float(count_products), f...  69.4 us
    pallas_call x3, Pallas kernels, exchange(): pl.pallas_call(functools.partial(exchange_kernel, n), out_shape=jax.Shape...  32.4 us
    sort x1, other arithmetic, body(): sid = lax.sort(firm_map)  5.74 us
    reduce_sum x1, other arithmetic, body(): jnp.sum(jnp.where(asked[:, None] == local[None, :], home[:, None], 0.0),...  3.98 us
    unnamed x9, local copies, waits for them, and re-layouts  3.73 us
    dot_general x1, matrix products, body(): got = jnp.dot(hot, caug, preferred_element_type=F32).astype(BF16)  3.68 us
    dot_general x1, matrix products, body(): jnp.dot(turn, both[:, :pp].reshape(LP, KA), preferred_element_type=F32)  3.52 us

profile of v1, /device:TPU:0, one launch (start us, length us, event | category | flops | bytes accessed | tf_op | source)
XLA Modules:
  0.0 139.3 jit_solution(17898367158002764276)
XLA Ops:
  0.6 0.1 pad.10.clone
  0.7 0.1 pad.13.clone
  0.8 0.7 broadcast_subtract_fusion.1
  1.5 5.7 %sort.14 = (s32[2048]{0:T(1024)}, s32[2048]{0:T(1024)}) sort(s32[2048]{0:T(1024)} %param.12, s32[2048]{0:T(1024)S(1)} %iota.8), dimensions={0}, to_apply=%region_0.0 | sort | flops 22528 | bytes 32768 | tf_op jit(solution)/shard_map/sort | solution.py:305
  7.2 9.6 %shard_map.94 = s32[8,1,256]{2,1,0:T(1,128)} custom-call(s32[8,1,256]{2,1,0:T(1,128)} %bitcast.32), custom_call_target="tpu_custom_call" | custom-call | tf_op jit(solution)/shard_map/pallas_call | solution.py:41
  16.9 0.7 broadcast_subtract_fusion
  17.6 0.7 fusion.13
  18.3 0.3 stack.14
  18.6 0.3 stack.13
  19.0 0.3 stack.12
  19.3 0.1 broadcast_in_dim.54
  19.4 2.5 %concatenate.19 = bf16[2048,256]{1,0:T(8,128)(2,1)S(1)} concatenate(bf16[2048,128]{1,0:T(8,128)(2,1)} %param.9, bf16[2048,1]{1,0:T(8,128)(2,1)S(1)} %stack.12, bf16[2048,1]{1,0:T(8,128)(2,1)S(1)} %stack.13, bf16[2048,1]{1,0:T(8,128)(2,1)S(1)} %stack.14, bf16[2048,125]{1,0:T(8,128)(2,1)S(1)} %broadcast_in_dim.54), dimensions={1} | concatenate | bytes 2097152 | tf_op jit(solution)/shard_map/concatenate | solution.py:309
  21.9 3.7 %fusion.7 = bf16[2304,256]{1,0:T(8,128)(2,1)S(1)} fusion(bf16[2048,256]{1,0:T(8,128)(2,1)S(1)} %concatenate.19, s32[2304]{0:T(1024)S(1)} %pad_add_fusion), kind=kOutput, calls=%fused_computation.11 | convolution fusion | flops 2421227520 | bytes 2237440 | tf_op jit(solution)/shard_map/dot_general | solution.py:314
  25.6 0.1 slice.44
  25.7 0.1 fusion.12
  25.8 0.1 fusion.11
  25.9 0.3 copy.25
  26.3 1.0 maximum_maximum_fusion.2.x_ref
  27.3 15.0 %shard_map.95 = bf16[8,304,128]{2,1,0:T(8,128)(2,1)} custom-call(bf16[8,304,128]{2,1,0:T(8,128)(2,1)} %maximum_maximum_fusion.2.x_ref), custom_call_target="tpu_custom_call" | custom-call | tf_op jit(solution)/shard_map/pallas_call | solution.py:41
  42.3 0.0 slice-start
  42.4 0.8 slice.38
  43.2 0.3 copy.24
  43.6 0.0 slice-done
  43.6 0.0 copy-start.1
  43.6 0.0 copy-start.2
  43.6 0.3 maximum_maximum_fusion.1
  43.9 0.6 convert_reduce_fusion.colpart
  44.5 0.1 slice.49
  44.6 0.0 copy-done.1
  44.6 0.0 copy-done.2
  44.6 0.0 copy-start
  44.6 3.5 %fusion.8.C = bf16[2048,256]{1,0:T(8,128)(2,1)} fusion(bf16[2048,256]{1,0:T(8,128)(2,1)S(1)} %bitcast.25, s32[2048]{0:T(1024)S(1)} %copy-done.2, s32[2048]{0:T(1024)S(1)} %copy-done.1), kind=kOutput, calls=%fused_computation.12 | convolution fusion | flops 2152202240 | bytes 2113536 | tf_op jit(solution)/shard_map/dot_general | solution.py:328
  48.1 1.4 copy.23.ids
  49.5 0.0 copy-done
  49.5 1.6 %maximum_maximum_fusion.T = bf16[4096,256]{1,0:T(8,128)(2,1)} fusion(bf16[4096,128]{1,0:T(8,128)(2,1)S(1)} %copy-done, bf16[256]{0:T(256)(128)(2,1)S(1)} %pad.10.clone, bf16[256]{0:T(256)(128)(2,1)S(1)} %pad.6.clone), kind=kLoop, calls=%fused_computation.13 | loop fusion | flops 6291456 | bytes 3146752 | tf_op jit(solution)/shard_map/concatenate | solution.py:329
  51.1 69.4 %shard_map.96 = (f32[2048,256]{1,0:T(8,128)}, f32[2,2048]{1,0:T(2,128)}) custom-call(bf16[2048,256]{1,0:T(8,128)(2,1)} %fusion.8.C, bf16[4096,256]{1,0:T(8,128)(2,1)} %maximum_maximum_fusion.T, f32[1,4096]{1,0:T(1,128)} %bitcast.31, f32[32,256]{1,0:T(8,128)} %convert_reduce_fusion.colpart, f32[16,128,128]{2,1,0:T(8,128)} %inv.1, s32[2048,1]{1,0:T(8,128)} %copy.23.ids, ...), custom_call_target="tpu_custom_call" | custom-call | tf_op jit(solution)/shard_map/pallas_call | solution.py:255
  120.5 1.4 %fusion.14 = (f32[1,2048]{1,0:T(1,128)}, f32[1,2048]{1,0:T(1,128)S(1)}) fusion(f32[2,2048]{1,0:T(2,128)} %get-tuple-element.8), kind=kLoop, calls=%fused_computation.30 | loop fusion | bytes 32768 | tf_op jit(solution)/shard_map/slice | solution.py:340
  122.0 2.6 %fusion.3 = f32[2048]{0:T(1024)} fusion(f32[2048]{0:T(1024)S(1)} %bitcast.36, s32[2048]{0:T(1024)S(1)} %copy-done.2, s32[2048]{0:T(1024)S(1)} %copy-done.1), kind=kLoop, calls=%fused_computation.5 | loop fusion | flops 12580864 | bytes 32768 | tf_op jit(solution)/shard_map/reduce_sum | solution.py:336
  124.5 7.7 %shard_map.97 = f32[8,1,256]{2,1,0:T(1,128)} custom-call(f32[8,1,256]{2,1,0:T(1,128)} %bitcast.33), custom_call_target="tpu_custom_call" | custom-call | tf_op jit(solution)/shard_map/pallas_call | solution.py:41
  132.3 4.0 %select_reduce_fusion = f32[2048]{0:T(1024)} fusion(f32[2048]{0:T(1024)} %bitcast.34, s32[2048]{0:T(1024)S(1)} %bitcast.29), kind=kLoop, calls=%fused_computation.6 | loop fusion | flops 12580864 | bytes 24576 | tf_op jit(solution)/shard_map/reduce_sum | solution.py:339
  136.3 3.0 %copy.27 = f32[2048,256]{1,0:T(8,128)} copy(f32[2048,256]{1,0:T(8,128)} %get-tuple-element.20) | data formatting | bytes 4194304
  (10 shorter events, 0.1 us)
Async XLA Ops:
  42.3 1.2 slice-start
  43.6 1.0 copy-start.1
  43.6 1.0 copy-start.2
  44.6 4.9 %copy-start = (bf16[4096,128]{1,0:T(8,128)(2,1)S(1)}, bf16[4096,128]{1,0:T(8,128)(2,1)}, u32[]{:S(2)}) copy-start(bf16[4096,128]{1,0:T(8,128)(2,1)} %param.7) | copy-start | bytes 3145732

commit v2 on v1

--- a/solution.py
+++ b/solution.py
@@ -52,11 +52,61 @@
     )(x)
 
 
+def shared_exchange_kernel(n, x_ref, o_ref, ssem, rsem, fs, fr, lsem):
+    me = lax.axis_index("prod")
+    cons = lax.axis_index("cons")
+    core = lax.rem(cons, 2)
+    partner = cons + 1 - 2 * core
+    span = x_ref.shape[1] // 2
+    part = pl.ds(pl.multiple_of(core * span, span), span)
+    barrier = pltpu.get_barrier_semaphore()
+    for d in range(1, n):
+        pl.semaphore_signal(barrier, inc=1, device_id={"prod": lax.rem(me + d, n)}, device_id_type=MESH)
+    pl.semaphore_signal(barrier, inc=1, device_id={"cons": partner}, device_id_type=MESH)
+    pl.semaphore_wait(barrier, n)
+    copies = []
+    for d in range(1, n):
+        peer = lax.rem(me + d, n)
+        copy = pltpu.make_async_remote_copy(
+            x_ref.at[peer, part], o_ref.at[me, part], ssem.at[d], rsem.at[d],
+            device_id={"prod": peer}, device_id_type=MESH,
+        )
+        copy.start()
+        copies.append(copy)
+    own = pltpu.make_async_copy(x_ref.at[me], o_ref.at[me], lsem)
+    own.start()
+    passed = []
+    for d in range(1, n):
+        copies[d - 1].wait()
+        source = lax.rem(me + n - d, n)
+        copy = pltpu.make_async_remote_copy(
+            o_ref.at[source, part], o_ref.at[source, part], fs.at[d], fr.at[d],
+            device_id={"cons": partner}, device_id_type=MESH,
+        )
+        copy.start()
+        passed.append(copy)
+    own.wait()
+    for copy in passed:
+        copy.wait()
+
+
+def shared_exchange(x, cid):
+    n = x.shape[0]
+    return pl.pallas_call(
+        functools.partial(shared_exchange_kernel, n),
+        out_shape=jax.ShapeDtypeStruct(x.shape, x.dtype),
+        in_specs=[VMEM],
+        out_specs=VMEM,
+        scratch_shapes=[pltpu.SemaphoreType.DMA((n,))] * 4 + [pltpu.SemaphoreType.DMA(())],
+        compiler_params=pltpu.CompilerParams(collective_id=cid, has_side_effects=True),
+    )(x)
+
+
 def main_kernel(
-    n, count_products, count_consumers, IC, JT,
-    C, T, coef, colpart, inv, ids, cols,
+    n, count_products, count_consumers, IC, JT, GR,
+    C, tastes, coef, colpart, inv, ids, cols,
     out, sm,
-    E, MS, CC, FL, WT, PO, PX, PR, YS, YR, ST,
+    T, SCB, SH, DG, E, MS, CC, FL, WT, PO, PX, PR, YS, YR, ST,
     ms_s, ms_r, cc_s, cc_r, px_s, px_r, y_s, y_r, st_s, st_r, o_s, o_r,
 ):
     me = lax.axis_index("prod")
@@ -65,7 +115,7 @@
     partner = cons + 1 - 2 * core
     across = lax.rem(cons + 2, 4)
     LP = C.shape[0]
-    LI = T.shape[0]
+    LI, K = tastes.shape
     nc, nt = LI // IC, LP // JT
     half = out.shape[1] // 2
     block = inv.shape[1]
@@ -96,6 +146,9 @@
         lax.fori_loop(1, n, step, 0)
 
     each_peer(lambda d: cc_copy(d).start())
+    T[:, :K] = tastes[...]
+    lane = lax.broadcasted_iota(jnp.int32, (LI, C.shape[1] - K), 1)
+    T[:, K:] = jnp.where(lane < 3, 1.0, 0.0).astype(BF16)
     CC[me] = colpart[...]
 
     def pass_one(ic, carry):
@@ -182,25 +235,29 @@
     def panel(jt, carry):
         rows = pl.ds(pl.multiple_of(jt * JT, JT), JT)
 
-        def over(ic, state):
-            acc, sh, dg = state
-            i0 = pl.multiple_of(ic * IC, IC)
-            sc = E[rows, pl.ds(i0, IC)] * FL[:, pl.ds(i0, IC)]
-            acc = acc + jnp.dot(sc.astype(BF16), WT[pl.ds(i0, IC), :], preferred_element_type=F32)
-            cs = sc * coef[:, pl.ds(i0, IC)]
-            for b in range(IC // 128):
-                sh = sh + sc[:, b * 128:(b + 1) * 128]
-                dg = dg + cs[:, b * 128:(b + 1) * 128]
-            return acc, sh, dg
-
-        zero = jnp.zeros((JT, 128), F32)
-        acc, sh, dg = lax.fori_loop(0, nc, over, (jnp.zeros((JT, 2 * half), F32), zero, zero))
+        def group(g, carry):
+            g0 = pl.multiple_of(g * GR, GR)
+            band = pl.ds(pl.multiple_of(jt * JT + g * GR, GR), GR)
+            sh = jnp.zeros((GR, 128), F32)
+            dg = jnp.zeros((GR, 128), F32)
+            for b in range(LI // 128):
+                at = pl.ds(b * 128, 128)
+                sc = E[band, at] * FL[:, at]
+                SCB[pl.ds(g0, GR), at] = sc.astype(BF16)
+                sh = sh + sc
+                dg = dg + sc * coef[:, at]
+            SH[pl.ds(g0, GR), :] = sh
+            DG[pl.ds(g0, GR), :] = dg
+            return carry
+
+        lax.fori_loop(0, JT // GR, group, 0)
+        acc = jnp.dot(SCB[...], WT[...], preferred_element_type=F32)
         first, second = acc[:, :half], acc[:, half:]
         PO[rows, :] = jnp.where(core == 0, first, second)
         PX[rows, :] = jnp.where(core == 0, second, first)
         px_copy(jt).start()
-        ST[cons, 0:1, rows] = jnp.sum(sh.T, axis=0, keepdims=True)
-        ST[cons, 1:2, rows] = jnp.sum(dg.T, axis=0, keepdims=True)
+        ST[cons, 0:1, rows] = jnp.sum(SH[...].T, axis=0, keepdims=True)
+        ST[cons, 1:2, rows] = jnp.sum(DG[...].T, axis=0, keepdims=True)
 
         @pl.when(jt > 0)
         def _():
@@ -227,7 +284,8 @@
             fb = jt * (JT // block) + b
             x = (YS[rows, :].astype(F32) + YR[rows, :].astype(F32)) / count_consumers
             diag = jnp.broadcast_to(ST[0, 1:2, rows], (half, block)).T
-            jac = x - jnp.where(ids[rows, :] == heads, diag, 0.0)
+            mine_ids = jnp.broadcast_to(ids[:, rows], (half, block)).T
+            jac = x - jnp.where(mine_ids == heads, diag, 0.0)
             m = inv[fb]
             out[rows, mine] = jnp.dot(m, jac, precision=lax.Precision.HIGHEST, preferred_element_type=F32)
             share8 = jnp.broadcast_to(sm[0:1, rows], (8, block))
@@ -245,19 +303,23 @@
     lax.fori_loop(0, nt, drain, 0)
 
 
-def run_main(n, caug, taug, coef, colpart, inverses, ids, cols, count_products, count_consumers):
-    LP, LI, W = caug.shape[0], taug.shape[0], cols.shape[1]
+def run_main(n, caug, tastes, coef, colpart, inverses, ids, cols, count_products, count_consumers):
+    LP, LI, W = caug.shape[0], tastes.shape[0], cols.shape[1]
     KA = caug.shape[1]
     IC, JT = min(512, LI), min(256, LP)
     nc, nt = LI // IC, LP // JT
     half = W // 2
     dma = pltpu.SemaphoreType.DMA
     return pl.pallas_call(
-        functools.partial(main_kernel, n, float(count_products), float(count_consumers), IC, JT),
+        functools.partial(main_kernel, n, float(count_products), float(count_consumers), IC, JT, min(32, JT)),
         out_shape=(jax.ShapeDtypeStruct((LP, W), F32), jax.ShapeDtypeStruct((2, LP), F32)),
         in_specs=[VMEM] * 7,
         out_specs=(VMEM, VMEM),
         scratch_shapes=[
+            pltpu.VMEM((LI, KA), BF16),
+            pltpu.VMEM((JT, LI), BF16),
+            pltpu.VMEM((JT, 128), F32),
+            pltpu.VMEM((JT, 128), F32),
             pltpu.VMEM((LP, LI), F32),
             pltpu.VMEM((n, nc, 2, IC), F32),
             pltpu.VMEM((n, W // n, KA), F32),
@@ -276,7 +338,7 @@
         compiler_params=pltpu.CompilerParams(
             collective_id=7, has_side_effects=True, vmem_limit_bytes=LIMIT
         ),
-    )(caug, taug, coef, colpart, inverses, ids, cols)
+    )(caug, tastes, coef, colpart, inverses, ids, cols)
 
 
 def split_mean(mean):
@@ -318,20 +380,17 @@
     means = jnp.pad(mine[:, :, K:K + 3].transpose(0, 2, 1), ((0, 0), (0, 0), (0, wide - each)))
     means = means.reshape(n, 3 * wide // 128, 128)
     total = each + means.shape[1]
-    fill = -(-total // 16) * 16 - total
+    fill = -(-total // 32) * 32 - total
     sent = jnp.concatenate([mine[:, :, :K], means, jnp.zeros((n, fill, K), BF16)], axis=1)
-    back = exchange(sent, 2)
+    back = shared_exchange(sent, 2)
     means_back = back[:, each:total].reshape(n, 3, wide)[:, :, :each].transpose(0, 2, 1)
     both = jnp.concatenate([back[:, :each], means_back, jnp.zeros((n, each, KA - K - 3), BF16)], axis=2)
     colpart = jnp.sum(both[:, pp:].astype(F32), axis=0)
     turn = (firm_map[:, None] == sid[None, :]).astype(BF16)
     cfirm = jnp.dot(turn, both[:, :pp].reshape(LP, KA), preferred_element_type=F32).astype(BF16)
-    taug = jnp.concatenate(
-        [tastes, jnp.ones((LI, 3), BF16), jnp.zeros((LI, KA - K - 3), BF16)], axis=1
-    )
     response, sm = run_main(
-        n, cfirm, taug, price_coef[None, :], colpart, inverses,
-        firm_map[:, None], panel_cols[None, :], count_products, count_consumers,
+        n, cfirm, tastes, price_coef[None, :], colpart, inverses,
+        firm_map.astype(F32)[None, :], panel_cols.astype(F32)[None, :], count_products, count_consumers,
     )
     values = jnp.sum(jnp.where(firm_map[:, None] == sid[None, :], sm[0][:, None], 0.0), axis=0)
     values = jnp.pad(values.reshape(n, 1, pp), ((0, 0), (0, 0), (0, lanes(pp) - pp)))

time: 140 us -> 127 us (0.907)
  Pallas kernels: 102 us -> 90 us
    pallas_call x3 -> x2, Pallas kernels: 32.4 us -> 17.3 us  [exchange(): pl.pallas_call(functools.partial(exchange_kernel, n), out_shape=jax.Shape...]
    pallas_call x0 -> x1, Pallas kernels: none -> 13.3 us  [shared_exchange(): pl.pallas_call(functools.partial(shared_exchange_kernel, n), out_shape=ja...]
    pallas_call x1, Pallas kernels: 69.4 us -> 59.4 us  [run_main(): pl.pallas_call(functools.partial(main_kernel, n, float(count_products), f...]
    convert_element_type x0 -> x2, other arithmetic: none -> 2.61 us  [the longest x1 1.32 us: body(): panel_cols.astype(F32)[None, :]]
    concatenate x1 -> x0, other arithmetic: 1.62 us -> none  [body(): jnp.concatenate([tastes, jnp.ones((LI, 3), BF16), jnp.zeros((LI, KA - K -...]
    unnamed x9 -> x7, local copies, waits for them, and re-layouts: 3.73 us -> 3.73 us
where the time goes in v2:
time: 127 us; the launch traced here: 126 us
  Pallas kernels  90 us (71%)
  other arithmetic  18.5 us (15%)
  local copies, waits for them, and re-layouts  9.95 us (8%)
  matrix products  7.18 us (6%)
    pallas_call x1, Pallas kernels, run_main(): pl.pallas_call(functools.partial(main_kernel, n, float(count_products), f...  59.4 us
    pallas_call x2, Pallas kernels, exchange(): pl.pallas_call(functools.partial(exchange_kernel, n), out_shape=jax.Shape...  17.3 us
    pallas_call x1, Pallas kernels, shared_exchange(): pl.pallas_call(functools.partial(shared_exchange_kernel, n), out_shape=ja...  13.3 us
    sort x1, other arithmetic, body(): sid = lax.sort(firm_map)  5.74 us
    reduce_sum x1, other arithmetic, body(): jnp.sum(jnp.where(asked[:, None] == local[None, :], home[:, None], 0.0),...  3.98 us
    unnamed x7, local copies, waits for them, and re-layouts  3.73 us
    dot_general x1, matrix products, body(): got = jnp.dot(hot, caug, preferred_element_type=F32).astype(BF16)  3.68 us
    dot_general x1, matrix products, body(): jnp.dot(turn, both[:, :pp].reshape(LP, KA), preferred_element_type=F32)  3.5 us

profile of v2, /device:TPU:0, one launch (start us, length us, event | category | flops | bytes accessed | tf_op | source)
XLA Modules:
  0.0 126.5 jit_solution(3391409118711864064)
XLA Ops:
  0.6 0.1 pad.7.clone
  0.7 0.1 pad.10.clone
  0.8 1.3 %fusion.15 = (f32[256]{0:T(256)}, s32[256]{0:T(256)S(1)}) fusion(s32[256]{0:T(256)} %param.11, s32[]{:T(128)S(6)} %mul.3), kind=kLoop, calls=%fused_computation.30 | loop fusion | flops 512 | bytes 3076 | tf_op jit(solution)/shard_map/convert_element_type | solution.py:393
  2.1 1.3 %convert_element_type.34 = f32[2048]{0:T(1024)} convert(s32[2048]{0:T(1024)} %param.12) | non-fusion elementwise | flops 2048 | bytes 16384 | tf_op jit(solution)/shard_map/convert_element_type | solution.py:393
  3.4 5.7 %sort.14 = (s32[2048]{0:T(1024)}, s32[2048]{0:T(1024)}) sort(s32[2048]{0:T(1024)} %param.12, s32[2048]{0:T(1024)S(1)} %iota.8), dimensions={0}, to_apply=%region_0.0 | sort | flops 22528 | bytes 32768 | tf_op jit(solution)/shard_map/sort | solution.py:367
  9.2 9.6 %shard_map.94 = s32[8,1,256]{2,1,0:T(1,128)} custom-call(s32[8,1,256]{2,1,0:T(1,128)} %bitcast.32), custom_call_target="tpu_custom_call" | custom-call | tf_op jit(solution)/shard_map/pallas_call | solution.py:41
  18.8 0.7 broadcast_subtract_fusion
  19.5 0.7 fusion.13
  20.2 0.3 stack.14
  20.5 0.3 stack.13
  20.9 0.3 stack.12
  21.2 0.1 broadcast_in_dim.48
  21.3 2.5 %concatenate.16 = bf16[2048,256]{1,0:T(8,128)(2,1)S(1)} concatenate(bf16[2048,128]{1,0:T(8,128)(2,1)} %param.9, bf16[2048,1]{1,0:T(8,128)(2,1)S(1)} %stack.12, bf16[2048,1]{1,0:T(8,128)(2,1)S(1)} %stack.13, bf16[2048,1]{1,0:T(8,128)(2,1)S(1)} %stack.14, bf16[2048,125]{1,0:T(8,128)(2,1)S(1)} %broadcast_in_dim.48), dimensions={1} | concatenate | bytes 2097152 | tf_op jit(solution)/shard_map/concatenate | solution.py:371
  23.8 3.7 %fusion.7 = bf16[2304,256]{1,0:T(8,128)(2,1)S(1)} fusion(bf16[2048,256]{1,0:T(8,128)(2,1)S(1)} %concatenate.16, s32[2304]{0:T(1024)S(1)} %pad_add_fusion), kind=kOutput, calls=%fused_computation.11 | convolution fusion | flops 2421227520 | bytes 2237440 | tf_op jit(solution)/shard_map/dot_general | solution.py:376
  27.5 0.1 slice.44
  27.6 0.1 fusion.12
  27.7 0.1 fusion.11
  27.8 0.3 copy.23
  28.2 1.1 maximum_maximum_fusion.1.x_ref
  29.3 13.3 %shard_map.95 = bf16[8,320,128]{2,1,0:T(8,128)(2,1)} custom-call(bf16[8,320,128]{2,1,0:T(8,128)(2,1)} %maximum_maximum_fusion.1.x_ref), custom_call_target="tpu_custom_call" | custom-call | tf_op jit(solution)/shard_map/pallas_call | solution.py:95
  42.6 0.0 slice-start
  42.6 0.8 slice.38
  43.4 0.3 copy.22
  43.8 0.0 slice-done
  43.8 0.0 copy-start
  43.8 0.0 copy-start.1
  43.8 0.3 maximum_maximum_fusion
  44.1 0.6 convert_reduce_fusion.colpart
  44.7 0.1 slice.49
  44.8 0.0 copy-done
  44.8 0.0 copy-done.1
  44.8 3.5 %fusion.8.C = bf16[2048,256]{1,0:T(8,128)(2,1)} fusion(bf16[2048,256]{1,0:T(8,128)(2,1)S(1)} %bitcast.25, s32[2048]{0:T(1024)S(1)} %copy-done.1, s32[2048]{0:T(1024)S(1)} %copy-done), kind=kOutput, calls=%fused_computation.12 | convolution fusion | flops 2152202240 | bytes 2113536 | tf_op jit(solution)/shard_map/dot_general | solution.py:390
  48.3 59.4 %shard_map.96 = (f32[2048,256]{1,0:T(8,128)}, f32[2,2048]{1,0:T(2,128)}) custom-call(bf16[2048,256]{1,0:T(8,128)(2,1)} %fusion.8.C, bf16[4096,128]{1,0:T(8,128)(2,1)} %tastes.1, f32[1,4096]{1,0:T(1,128)} %bitcast.31, f32[32,256]{1,0:T(8,128)} %convert_reduce_fusion.colpart, f32[16,128,128]{2,1,0:T(8,128)} %inv.1, f32[1,2048]{1,0:T(1,128)} %bitcast.27, ...), custom_call_target="tpu_custom_call" | custom-call | tf_op jit(solution)/shard_map/pallas_call | solution.py:313
  107.7 1.4 %fusion.14 = (f32[1,2048]{1,0:T(1,128)}, f32[1,2048]{1,0:T(1,128)S(1)}) fusion(f32[2,2048]{1,0:T(2,128)} %get-tuple-element.8), kind=kLoop, calls=%fused_computation.29 | loop fusion | bytes 32768 | tf_op jit(solution)/shard_map/slice | solution.py:399
  109.1 2.6 %fusion.3 = f32[2048]{0:T(1024)} fusion(f32[2048]{0:T(1024)S(1)} %bitcast.36, s32[2048]{0:T(1024)S(1)} %copy-done.1, s32[2048]{0:T(1024)S(1)} %copy-done), kind=kLoop, calls=%fused_computation.5 | loop fusion | flops 12580864 | bytes 32768 | tf_op jit(solution)/shard_map/reduce_sum | solution.py:395
  111.7 7.7 %shard_map.97 = f32[8,1,256]{2,1,0:T(1,128)} custom-call(f32[8,1,256]{2,1,0:T(1,128)} %bitcast.33), custom_call_target="tpu_custom_call" | custom-call | tf_op jit(solution)/shard_map/pallas_call | solution.py:41
  119.5 4.0 %select_reduce_fusion = f32[2048]{0:T(1024)} fusion(f32[2048]{0:T(1024)} %bitcast.34, s32[2048]{0:T(1024)S(1)} %bitcast.29), kind=kLoop, calls=%fused_computation.6 | loop fusion | flops 12580864 | bytes 24576 | tf_op jit(solution)/shard_map/reduce_sum | solution.py:398
  123.4 3.0 %copy.25 = f32[2048,256]{1,0:T(8,128)} copy(f32[2048,256]{1,0:T(8,128)} %get-tuple-element.22) | data formatting | bytes 4194304
  (8 shorter events, 0.1 us)
Async XLA Ops:
  42.6 1.2 slice-start
  43.8 1.0 copy-start
  43.8 1.0 copy-start.1

commit v3 on v2

--- a/solution.py
+++ b/solution.py
@@ -14,100 +14,208 @@
 LIMIT = 63 * 1024 * 1024
 
 
-def exchange_kernel(n, x_ref, o_ref, ssem, rsem, lsem):
-    me = lax.axis_index("prod")
-    barrier = pltpu.get_barrier_semaphore()
-    for d in range(1, n):
-        pl.semaphore_signal(barrier, inc=1, device_id={"prod": lax.rem(me + d, n)}, device_id_type=MESH)
-    pl.semaphore_wait(barrier, n - 1)
-    copies = []
-    for d in range(1, n):
-        peer = lax.rem(me + d, n)
-        copy = pltpu.make_async_remote_copy(
-            x_ref.at[peer], o_ref.at[me], ssem.at[d], rsem.at[d],
-            device_id={"prod": peer}, device_id_type=MESH,
-        )
-        copy.start()
-        copies.append(copy)
-    own = pltpu.make_async_copy(x_ref.at[me], o_ref.at[me], lsem)
-    own.start()
-    own.wait()
-    for copy in copies:
-        copy.wait()
-
-
-def exchange(x, cid):
-    n = x.shape[0]
-    return pl.pallas_call(
-        functools.partial(exchange_kernel, n),
-        out_shape=jax.ShapeDtypeStruct(x.shape, x.dtype),
-        in_specs=[VMEM],
-        out_specs=VMEM,
-        scratch_shapes=[
-            pltpu.SemaphoreType.DMA((n,)),
-            pltpu.SemaphoreType.DMA((n,)),
-            pltpu.SemaphoreType.DMA(()),
-        ],
-        compiler_params=pltpu.CompilerParams(collective_id=cid, has_side_effects=True),
-    )(x)
-
-
-def shared_exchange_kernel(n, x_ref, o_ref, ssem, rsem, fs, fr, lsem):
+def turned(row):
+    return jnp.broadcast_to(row, (128, 128)).T
+
+
+def prep_kernel(
+    n, LP, cp,
+    sid, fm, chars, mean, cols,
+    C, colpart, colmean, asked,
+    CA, X, XM, XC, XCM, R, RM, RC, RCM,
+    a_s, a_r, x_s, x_r, f_s, f_r, m_s, m_r, c_s, c_r, k_s, k_r,
+):
     me = lax.axis_index("prod")
     cons = lax.axis_index("cons")
     core = lax.rem(cons, 2)
     partner = cons + 1 - 2 * core
-    span = x_ref.shape[1] // 2
-    part = pl.ds(pl.multiple_of(core * span, span), span)
+    K = chars.shape[1]
+    pad = sid.shape[2]
+    base = me * LP
     barrier = pltpu.get_barrier_semaphore()
     for d in range(1, n):
         pl.semaphore_signal(barrier, inc=1, device_id={"prod": lax.rem(me + d, n)}, device_id_type=MESH)
     pl.semaphore_signal(barrier, inc=1, device_id={"cons": partner}, device_id_type=MESH)
+
+    CA[:, :K] = chars[...]
+    lane = lax.broadcasted_iota(jnp.int32, (128, K), 1)
+
+    def split(column):
+        a = column.astype(BF16).astype(F32)
+        b = (column - a).astype(BF16).astype(F32)
+        c = column - a - b
+        return jnp.where(lane == 0, a, jnp.where(lane == 1, b, jnp.where(lane == 2, c, 0.0))).astype(BF16)
+
+    def widen(g, carry):
+        rows = pl.ds(pl.multiple_of(g * 128, 128), 128)
+        CA[rows, K:] = split(turned(mean[:, rows]))
+        return carry
+
+    lax.fori_loop(0, LP // 128, widen, 0)
     pl.semaphore_wait(barrier, n)
-    copies = []
-    for d in range(1, n):
-        peer = lax.rem(me + d, n)
-        copy = pltpu.make_async_remote_copy(
-            x_ref.at[peer, part], o_ref.at[me, part], ssem.at[d], rsem.at[d],
-            device_id={"prod": peer}, device_id_type=MESH,
-        )
-        copy.start()
-        copies.append(copy)
-    own = pltpu.make_async_copy(x_ref.at[me], o_ref.at[me], lsem)
-    own.start()
-    passed = []
-    for d in range(1, n):
-        copies[d - 1].wait()
+
+    def send(src, dst, s, r, d):
+        return pltpu.make_async_remote_copy(
+            src, dst, s.at[d], r.at[d],
+            device_id={"prod": lax.rem(me + d, n)}, device_id_type=MESH,
+        )
+
+    span = pad // 2
+    part = pl.ds(pl.multiple_of(core * span, span), span)
+
+    def a_copy(d):
+        return send(sid.at[lax.rem(me + d, n)], asked.at[me], a_s, a_r, d)
+
+    def x_copy(d):
+        return send(X.at[lax.rem(me + d, n), part], R.at[me, part], x_s, x_r, d)
+
+    def m_copy(d):
+        return send(XM.at[lax.rem(me + d, n)], RM.at[me], m_s, m_r, d)
+
+    def c_copy(d):
+        return send(XC.at[lax.rem(me + d, n)], RC.at[me], c_s, c_r, d)
+
+    def k_copy(d):
+        return send(XCM, RCM.at[me], k_s, k_r, d)
+
+    def f_copy(d):
         source = lax.rem(me + n - d, n)
-        copy = pltpu.make_async_remote_copy(
-            o_ref.at[source, part], o_ref.at[source, part], fs.at[d], fr.at[d],
+        return pltpu.make_async_remote_copy(
+            R.at[source, part], R.at[source, part], f_s.at[d], f_r.at[d],
             device_id={"cons": partner}, device_id_type=MESH,
         )
-        copy.start()
-        passed.append(copy)
-    own.wait()
-    for copy in passed:
-        copy.wait()
-
-
-def shared_exchange(x, cid):
-    n = x.shape[0]
+
+    def loop(fn, lo=1):
+        def step(d, carry):
+            fn(d)
+            return carry
+        lax.fori_loop(lo, n, step, 0)
+
+    loop(lambda d: a_copy(d).start())
+    asked[me] = sid[me]
+
+    def pick(row):
+        want = turned((row - base).astype(F32))
+        spot = lax.broadcasted_iota(jnp.int32, (128, 128), 1).astype(F32)
+        hot = jnp.concatenate(
+            [jnp.where(want == spot + float(b * 128), 1.0, 0.0).astype(BF16) for b in range(LP // 128)], axis=1
+        )
+        got = jnp.dot(hot, CA[...], preferred_element_type=F32)
+        t = got[:, K:].T
+        return got[:, :K], t[0:1] + (t[1:2] + t[2:3])
+
+    for g in range(cols.shape[1] // 128):
+        at = pl.ds(g * 128, 128)
+        rows, means = pick(cols[:, at])
+        lots = 128 // cp
+        XC[g * lots:(g + 1) * lots, :cp, :] = rows.reshape(lots, cp, K).astype(BF16)
+        XCM[:, at] = means
+    loop(lambda d: c_copy(d).start())
+    loop(lambda d: k_copy(d).start())
+    RC[me] = XC[me]
+    RCM[me] = XCM[...]
+
+    def answer(d, carry):
+        source = lax.rem(me + n - d, n)
+
+        @pl.when(d > 0)
+        def _():
+            send(sid.at[source], asked.at[source], a_s, a_r, lax.rem(n - d, n)).wait_send()
+            send(sid.at[source], asked.at[source], a_s, a_r, d).wait_recv()
+
+        for b in range(pad // 128):
+            at = pl.ds(b * 128, 128)
+            rows, means = pick(asked[source, :, at])
+            X[source, at, :] = rows.astype(BF16)
+            XM[source, :, at] = means
+
+        @pl.when(d > 0)
+        def _():
+            back = lax.rem(n - d, n)
+            x_copy(back).start()
+            m_copy(back).start()
+
+        return carry
+
+    lax.fori_loop(0, n, answer, 0)
+    R[me] = X[me]
+    RM[me] = XM[me]
+
+    loop(lambda d: c_copy(d).wait())
+    loop(lambda d: k_copy(d).wait())
+    total = RC[0, :cp, :].astype(F32)
+    heads = RCM[0]
+    for p in range(1, n):
+        total = total + RC[p, :cp, :].astype(F32)
+        heads = heads + RCM[p]
+    colpart[...] = total
+    colmean[...] = heads
+
+    def relay(d):
+        x_copy(d).wait()
+        f_copy(d).start()
+
+    loop(relay)
+    loop(lambda d: m_copy(d).wait())
+    loop(lambda d: f_copy(d).wait())
+    table = R[...].reshape(n * pad, K)
+
+    def firm(g, carry):
+        rows = pl.ds(pl.multiple_of(g * 128, 128), 128)
+        want = turned(fm[:, rows].astype(F32))
+        hots = []
+        mid = jnp.zeros((128, 128), F32)
+        for p in range(n):
+            for b in range(pad // 128):
+                at = pl.ds(b * 128, 128)
+                hit = want == sid[p, :, at].astype(F32)
+                hots.append(jnp.where(hit, 1.0, 0.0).astype(BF16))
+                mid = mid + jnp.where(hit, RM[p, :, at], 0.0)
+        C[rows, :K] = jnp.dot(jnp.concatenate(hots, axis=1), table, preferred_element_type=F32).astype(BF16)
+        C[rows, K:] = split(jnp.sum(mid, axis=1, keepdims=True))
+        return carry
+
+    lax.fori_loop(0, LP // 128, firm, 0)
+
+
+def prepare(n, sid, fm, chars, mean, cols):
+    LP, K = chars.shape
+    W = cols.shape[1]
+    cp = W // n
+    room = -(-cp // 16) * 16
+    pad = sid.shape[2]
+    dma = pltpu.SemaphoreType.DMA
     return pl.pallas_call(
-        functools.partial(shared_exchange_kernel, n),
-        out_shape=jax.ShapeDtypeStruct(x.shape, x.dtype),
-        in_specs=[VMEM],
-        out_specs=VMEM,
-        scratch_shapes=[pltpu.SemaphoreType.DMA((n,))] * 4 + [pltpu.SemaphoreType.DMA(())],
-        compiler_params=pltpu.CompilerParams(collective_id=cid, has_side_effects=True),
-    )(x)
+        functools.partial(prep_kernel, n, LP, cp),
+        out_shape=(
+            jax.ShapeDtypeStruct((LP, 2 * K), BF16),
+            jax.ShapeDtypeStruct((cp, K), F32),
+            jax.ShapeDtypeStruct((1, W), F32),
+            jax.ShapeDtypeStruct(sid.shape, jnp.int32),
+        ),
+        in_specs=[VMEM] * 5,
+        out_specs=(VMEM,) * 4,
+        scratch_shapes=[
+            pltpu.VMEM((LP, 2 * K), BF16),
+            pltpu.VMEM((n, pad, K), BF16),
+            pltpu.VMEM((n, 1, pad), F32),
+            pltpu.VMEM((n, room, K), BF16),
+            pltpu.VMEM((1, W), F32),
+            pltpu.VMEM((n, pad, K), BF16),
+            pltpu.VMEM((n, 1, pad), F32),
+            pltpu.VMEM((n, room, K), BF16),
+            pltpu.VMEM((n, 1, W), F32),
+        ] + [dma((n,))] * 12,
+        compiler_params=pltpu.CompilerParams(collective_id=1, has_side_effects=True),
+    )(sid, fm, chars, mean, cols)
 
 
 def main_kernel(
     n, count_products, count_consumers, IC, JT, GR,
-    C, tastes, coef, colpart, inv, ids, cols,
+    C, tastes, coef, colpart, colmean, inv, ids, cols, sid, asked,
     out, sm,
-    T, SCB, SH, DG, E, MS, CC, FL, WT, PO, PX, PR, YS, YR, ST,
-    ms_s, ms_r, cc_s, cc_r, px_s, px_r, y_s, y_r, st_s, st_r, o_s, o_r,
+    SV, HV, T, SCB, SH, DG, E, MS, CC, FL, WT, PO, PX, PR, YS, YR, ST,
+    ms_s, ms_r, cc_s, cc_r, px_s, px_r, y_s, y_r, st_s, st_r, o_s, o_r, h_s, h_r,
 ):
     me = lax.axis_index("prod")
     cons = lax.axis_index("cons")
@@ -179,6 +287,7 @@
     lax.fori_loop(0, nc, pass_one, 0)
     each_peer(lambda d: cc_copy(d).wait())
     ccv = CC[...].reshape(CC.shape[0] * CC.shape[1], CC.shape[2]).astype(BF16)
+    cm = jnp.concatenate([turned(colmean[:, g * 128:(g + 1) * 128])[:, :1] for g in range(colmean.shape[1] // 128)], axis=0)
 
     def weights(ic, carry):
         each_peer(lambda d: ms_copy(d, ic).wait())
@@ -191,7 +300,7 @@
             den = den + MS[d, ic, 1:2, :] * jnp.exp(MS[d, ic, 0:1, :] - peak)
         f = count_products / den
         FL[:, pl.ds(i0, IC)] = jnp.exp(MS[0, ic, 0:1, :] - peak) * f
-        cu = lax.dot_general(ccv, T[pl.ds(i0, IC), :], NT, preferred_element_type=F32)
+        cu = lax.dot_general(ccv, tastes[pl.ds(i0, IC), :], NT, preferred_element_type=F32) + cm
         w = coef[:, pl.ds(i0, IC)] * (f * jnp.exp(cu - peak))
         WT[pl.ds(i0, IC), :] = w.T.astype(BF16)
         return carry
@@ -273,6 +382,31 @@
         st_copy(d).wait()
     sm[0:1, :] = (ST[0, 0:1, :] + ST[1, 0:1, :] + ST[2, 0:1, :] + ST[3, 0:1, :]) / count_consumers
     ST[0, 1:2, :] = (ST[0, 1:2, :] + ST[1, 1:2, :] + ST[2, 1:2, :] + ST[3, 1:2, :]) / count_consumers
+    pad = sid.shape[2]
+    spans = [(p, b) for p in range(n) for b in range(pad // 128)]
+
+    def sorted_step(g, carry):
+        rows = pl.ds(pl.multiple_of(g * 128, 128), 128)
+        want = turned(ids[:, rows])
+        share = turned(sm[0:1, rows])
+        for p, b in spans:
+            at = pl.ds(b * 128, 128)
+            hit = jnp.where(want == sid[p, :, at].astype(F32), share, 0.0)
+            SV[p, :, at] += jnp.sum(hit, axis=0, keepdims=True)
+        return carry
+
+    SV[...] = jnp.zeros_like(SV)
+    lax.fori_loop(0, LP // 128, sorted_step, 0)
+
+    def h_copy(d):
+        peer = lax.rem(me + d, n)
+        return pltpu.make_async_remote_copy(
+            SV.at[peer], HV.at[me], h_s.at[d], h_r.at[d],
+            device_id={"prod": peer}, device_id_type=MESH,
+        )
+
+    each_peer(lambda d: h_copy(d).start())
+    HV[me] = SV[me]
     mine = pl.ds(pl.multiple_of(core * half, half), half)
     heads = cols[:, mine]
 
@@ -296,6 +430,23 @@
 
     lax.fori_loop(0, nt, finish, 0)
 
+    each_peer(lambda d: h_copy(d).wait())
+    sm[2:3, :] = jnp.zeros((1, LP), F32)
+
+    def home_step(p, carry):
+        for b in range(pad // 128):
+            at = pl.ds(b * 128, 128)
+            want = turned((asked[p, :, at] - me * LP).astype(F32))
+            share = turned(HV[p, :, at])
+            spot = lax.broadcasted_iota(jnp.int32, (128, 128), 1).astype(F32)
+            for g in range(LP // 128):
+                to = pl.ds(g * 128, 128)
+                hit = jnp.where(want == spot + float(g * 128), share, 0.0)
+                sm[2:3, to] += jnp.sum(hit, axis=0, keepdims=True)
+        return carry
+
+    lax.fori_loop(0, n, home_step, 0)
+
     def drain(jt, carry):
         o_copy(jt).wait()
         return carry
@@ -303,7 +454,7 @@
     lax.fori_loop(0, nt, drain, 0)
 
 
-def run_main(n, caug, tastes, coef, colpart, inverses, ids, cols, count_products, count_consumers):
+def run_main(n, caug, tastes, coef, colpart, colmean, inverses, ids, cols, sid, asked, count_products, count_consumers):
     LP, LI, W = caug.shape[0], tastes.shape[0], cols.shape[1]
     KA = caug.shape[1]
     IC, JT = min(512, LI), min(256, LP)
@@ -312,17 +463,19 @@
     dma = pltpu.SemaphoreType.DMA
     return pl.pallas_call(
         functools.partial(main_kernel, n, float(count_products), float(count_consumers), IC, JT, min(32, JT)),
-        out_shape=(jax.ShapeDtypeStruct((LP, W), F32), jax.ShapeDtypeStruct((2, LP), F32)),
-        in_specs=[VMEM] * 7,
+        out_shape=(jax.ShapeDtypeStruct((LP, W), F32), jax.ShapeDtypeStruct((3, LP), F32)),
+        in_specs=[VMEM] * 10,
         out_specs=(VMEM, VMEM),
         scratch_shapes=[
+            pltpu.VMEM(sid.shape, F32),
+            pltpu.VMEM(sid.shape, F32),
             pltpu.VMEM((LI, KA), BF16),
             pltpu.VMEM((JT, LI), BF16),
             pltpu.VMEM((JT, 128), F32),
             pltpu.VMEM((JT, 128), F32),
             pltpu.VMEM((LP, LI), F32),
             pltpu.VMEM((n, nc, 2, IC), F32),
-            pltpu.VMEM((n, W // n, KA), F32),
+            pltpu.VMEM((n, W // n, KA // 2), F32),
             pltpu.VMEM((1, LI), F32),
             pltpu.VMEM((LI, W), BF16),
             pltpu.VMEM((LP, half), F32),
@@ -333,19 +486,12 @@
             pltpu.VMEM((4, 2, LP), F32),
             dma((n, nc)), dma((n, nc)), dma((n,)), dma((n,)),
             dma((nt,)), dma((nt,)), dma((nt,)), dma((nt,)),
-            dma((4,)), dma((4,)), dma((nt,)), dma((nt,)),
+            dma((4,)), dma((4,)), dma((nt,)), dma((nt,)), dma((n,)), dma((n,)),
         ],
         compiler_params=pltpu.CompilerParams(
             collective_id=7, has_side_effects=True, vmem_limit_bytes=LIMIT
         ),
-    )(caug, tastes, coef, colpart, inverses, ids, cols)
-
-
-def split_mean(mean):
-    a = lax.reduce_precision(mean, 8, 7)
-    b = lax.reduce_precision(mean - a, 8, 7)
-    c = mean - a - b
-    return jnp.stack([a.astype(BF16), b.astype(BF16), c.astype(BF16)], axis=1)
+    )(caug, tastes, coef, colpart, colmean, inverses, ids, cols, sid, asked)
 
 
 def lanes(count):
@@ -359,44 +505,19 @@
     W = panel_cols.shape[0]
     count_products = LP * n
     count_consumers = LI * lax.axis_size("cons")
-    pp, cp = LP // n, W // n
-    KA = 2 * K
-    base = lax.axis_index("prod") * LP
-    local = lax.iota(jnp.int32, LP)
-
-    sid = lax.sort(firm_map)
-    wanted = jnp.pad(sid.reshape(n, 1, pp), ((0, 0), (0, 0), (0, lanes(pp) - pp)))
-    asked = exchange(wanted, 1)[:, 0, :pp].reshape(LP) - base
-
-    caug = jnp.concatenate(
-        [characteristics, split_mean(mean_utility), jnp.zeros((LP, KA - K - 3), BF16)], axis=1
+    pp = LP // n
+    sid = jnp.pad(
+        lax.sort(firm_map).reshape(n, 1, pp), ((0, 0), (0, 0), (0, lanes(pp) - pp)), constant_values=-1
     )
-    picks = jnp.concatenate([asked, panel_cols - base])
-    hot = (picks[:, None] == local[None, :]).astype(BF16)
-    got = jnp.dot(hot, caug, preferred_element_type=F32).astype(BF16)
-    mine = jnp.concatenate([got[:LP].reshape(n, pp, KA), got[LP:].reshape(n, cp, KA)], axis=1)
-    each = pp + cp
-    wide = lanes(each)
-    means = jnp.pad(mine[:, :, K:K + 3].transpose(0, 2, 1), ((0, 0), (0, 0), (0, wide - each)))
-    means = means.reshape(n, 3 * wide // 128, 128)
-    total = each + means.shape[1]
-    fill = -(-total // 32) * 32 - total
-    sent = jnp.concatenate([mine[:, :, :K], means, jnp.zeros((n, fill, K), BF16)], axis=1)
-    back = shared_exchange(sent, 2)
-    means_back = back[:, each:total].reshape(n, 3, wide)[:, :, :each].transpose(0, 2, 1)
-    both = jnp.concatenate([back[:, :each], means_back, jnp.zeros((n, each, KA - K - 3), BF16)], axis=2)
-    colpart = jnp.sum(both[:, pp:].astype(F32), axis=0)
-    turn = (firm_map[:, None] == sid[None, :]).astype(BF16)
-    cfirm = jnp.dot(turn, both[:, :pp].reshape(LP, KA), preferred_element_type=F32).astype(BF16)
+    cfirm, colpart, colmean, asked = prepare(
+        n, sid, firm_map[None, :], characteristics, mean_utility[None, :], panel_cols[None, :]
+    )
     response, sm = run_main(
-        n, cfirm, tastes, price_coef[None, :], colpart, inverses,
-        firm_map.astype(F32)[None, :], panel_cols.astype(F32)[None, :], count_products, count_consumers,
+        n, cfirm, tastes, price_coef[None, :], colpart, colmean, inverses,
+        firm_map.astype(F32)[None, :], panel_cols.astype(F32)[None, :], sid, asked,
+        count_products, count_consumers,
     )
-    values = jnp.sum(jnp.where(firm_map[:, None] == sid[None, :], sm[0][:, None], 0.0), axis=0)
-    values = jnp.pad(values.reshape(n, 1, pp), ((0, 0), (0, 0), (0, lanes(pp) - pp)))
-    home = exchange(values, 3)[:, 0, :pp].reshape(LP)
-    shares = jnp.sum(jnp.where(asked[:, None] == local[None, :], home[:, None], 0.0), axis=0)
-    return shares, sm[1], response
+    return sm[2], sm[1], response
 
 
 def solution(mesh):

time: 127 us -> 104 us (0.82)
  other arithmetic: 18.5 us -> 8.29 us
  matrix products: 7.18 us -> 0 us
  local copies, waits for them, and re-layouts: 9.95 us -> 4.5 us
    reduce_sum x3 -> x0, other arithmetic: 7.19 us -> none  [the longest x1 3.98 us: body(): jnp.sum(jnp.where(asked[:, None] == local[None, :], home[:, None], 0.0),...]
    dot_general x2 -> x0, matrix products: 7.18 us -> none  [the longest x1 3.68 us: body(): got = jnp.dot(hot, caug, preferred_element_type=F32).astype(BF16)]
    pallas_call x1, Pallas kernels: 59.4 us -> 63 us  [run_main(): pl.pallas_call(functools.partial(main_kernel, n, float(count_products), f...]
    pallas_call x3 -> x1, Pallas kernels: 30.6 us -> 27.2 us  [prepare(): pl.pallas_call(functools.partial(prep_kernel, n, LP, cp), out_shape=(jax....]
    concatenate x3 -> x0, local copies, waits for them, and re-layouts: 2.68 us -> none  [the longest x1 2.53 us: body(): jnp.concatenate([characteristics, split_mean(mean_utility), jnp.zeros((LP...]
    concatenate x4 -> x0, other arithmetic: 1.44 us -> none  [the longest x1 1.05 us: body(): jnp.concatenate([mine[:, :, :K], means, jnp.zeros((n, fill, K), BF16)], a...]
    unnamed x7 -> x1, local copies, waits for them, and re-layouts: 3.73 us -> 3.04 us
where the time goes in v3:
time: 104 us
  Pallas kernels  90.3 us (87%)
  other arithmetic  8.29 us (8%)
  local copies, waits for them, and re-layouts  4.5 us (4%)
    pallas_call x1, Pallas kernels, run_main(): pl.pallas_call(functools.partial(main_kernel, n, float(count_products), f...  63 us
    pallas_call x1, Pallas kernels, prepare(): pl.pallas_call(functools.partial(prep_kernel, n, LP, cp), out_shape=(jax....  27.2 us
    sort x1, other arithmetic, body(): lax.sort(firm_map).reshape(n, 1, pp)  5.74 us
    unnamed x1, local copies, waits for them, and re-layouts  3.04 us

profile of v3, /device:TPU:0, one launch (start us, length us, event | category | flops | bytes accessed | tf_op | source)
XLA Modules:
  0.0 103.7 jit_solution(2225183881708940937)
XLA Ops:
  0.6 1.3 %convert_element_type.7 = f32[256]{0:T(256)} convert(s32[256]{0:T(256)} %param.11) | non-fusion elementwise | flops 256 | bytes 2048 | tf_op jit(solution)/shard_map/convert_element_type | solution.py:517
  1.9 1.3 %convert_element_type.6 = f32[2048]{0:T(1024)} convert(s32[2048]{0:T(1024)} %param.12) | non-fusion elementwise | flops 2048 | bytes 16384 | tf_op jit(solution)/shard_map/convert_element_type | solution.py:517
  3.2 5.7 %sort.14 = (s32[2048]{0:T(1024)}, s32[2048]{0:T(1024)}) sort(s32[2048]{0:T(1024)} %param.12, s32[2048]{0:T(1024)S(1)} %iota.3), dimensions={0}, to_apply=%region_0.0 | sort | flops 22528 | bytes 32768 | tf_op jit(solution)/shard_map/sort | solution.py:510
  8.9 27.2 %shard_map.94 = (bf16[2048,256]{1,0:T(8,128)(2,1)}, f32[32,128]{1,0:T(8,128)}, f32[1,256]{1,0:T(1,128)}, s32[8,1,256]{2,1,0:T(1,128)}) custom-call(s32[8,1,256]{2,1,0:T(1,128)} %bitcast.10, s32[1,2048]{1,0:T(1,128)} %bitcast.9, bf16[2048,128]{1,0:T(8,128)(2,1)} %chars.1, f32[1,2048]{1,0:T(1,128)} %bitcast.14, s32[1,256]{1,0:T(1,128)} %bitcast.17), custom_call_target="tpu_custom_call" | custom-call | tf_op jit(solution)/shard_map/pallas_call | solution.py:188
  36.2 63.0 %shard_map.95 = (f32[2048,256]{1,0:T(8,128)}, f32[3,2048]{1,0:T(4,128)}) custom-call(bf16[2048,256]{1,0:T(8,128)(2,1)} %get-tuple-element.12.C, bf16[4096,128]{1,0:T(8,128)(2,1)} %tastes.1, f32[1,4096]{1,0:T(1,128)} %bitcast.13, f32[32,128]{1,0:T(8,128)} %get-tuple-element.13.colpart, f32[1,256]{1,0:T(1,128)} %get-tuple-element.14.colmean, ...), custom_call_target="tpu_custom_call" | custom-call | tf_op jit(solution)/shard_map/pallas_call | solution.py:464
  99.2 1.5 %fusion = (f32[1,2048]{1,0:T(1,128)}, f32[1,2048]{1,0:T(1,128)}) fusion(f32[3,2048]{1,0:T(4,128)} %get-tuple-element.16), kind=kLoop, calls=%fused_computation | loop fusion | bytes 32768 | tf_op jit(solution)/shard_map/slice | solution.py:520
  100.7 3.0 %copy.11 = f32[2048,256]{1,0:T(8,128)} copy(f32[2048,256]{1,0:T(8,128)} %get-tuple-element.25) | data formatting | bytes 4194304
  (1 shorter events, 0.0 us)

commit v4 on v3

--- a/solution.py
+++ b/solution.py
@@ -161,21 +161,25 @@
     table = R[...].reshape(n * pad, K)
 
     def firm(g, carry):
-        rows = pl.ds(pl.multiple_of(g * 128, 128), 128)
-        want = turned(fm[:, rows].astype(F32))
-        hots = []
-        mid = jnp.zeros((128, 128), F32)
-        for p in range(n):
-            for b in range(pad // 128):
-                at = pl.ds(b * 128, 128)
-                hit = want == sid[p, :, at].astype(F32)
-                hots.append(jnp.where(hit, 1.0, 0.0).astype(BF16))
-                mid = mid + jnp.where(hit, RM[p, :, at], 0.0)
-        C[rows, :K] = jnp.dot(jnp.concatenate(hots, axis=1), table, preferred_element_type=F32).astype(BF16)
-        C[rows, K:] = split(jnp.sum(mid, axis=1, keepdims=True))
-        return carry
-
-    lax.fori_loop(0, LP // 128, firm, 0)
+        bands = []
+        for h in range(2):
+            rows = pl.ds(pl.multiple_of(g * 256 + h * 128, 128), 128)
+            want = turned(fm[:, rows].astype(F32))
+            hots = []
+            mid = jnp.zeros((128, 128), F32)
+            for p in range(n):
+                for b in range(pad // 128):
+                    at = pl.ds(b * 128, 128)
+                    hit = want == sid[p, :, at].astype(F32)
+                    hots.append(jnp.where(hit, 1.0, 0.0).astype(BF16))
+                    mid = mid + jnp.where(hit, RM[p, :, at], 0.0)
+            bands.append(jnp.concatenate(hots, axis=1))
+            C[rows, K:] = split(jnp.sum(mid, axis=1, keepdims=True))
+        rows = pl.ds(pl.multiple_of(g * 256, 256), 256)
+        C[rows, :K] = jnp.dot(jnp.concatenate(bands, axis=0), table, preferred_element_type=F32).astype(BF16)
+        return carry
+
+    lax.fori_loop(0, LP // 256, firm, 0)
 
 
 def prepare(n, sid, fm, chars, mean, cols):
@@ -387,7 +391,7 @@
 
     def sorted_step(g, carry):
         rows = pl.ds(pl.multiple_of(g * 128, 128), 128)
-        want = turned(ids[:, rows])
+        want = turned(ids[:, rows].astype(F32))
         share = turned(sm[0:1, rows])
         for p, b in spans:
             at = pl.ds(b * 128, 128)
@@ -408,7 +412,7 @@
     each_peer(lambda d: h_copy(d).start())
     HV[me] = SV[me]
     mine = pl.ds(pl.multiple_of(core * half, half), half)
-    heads = cols[:, mine]
+    heads = cols[:, mine].astype(F32)
 
     def finish(jt, carry):
         y_copy(jt).wait()
@@ -418,7 +422,7 @@
             fb = jt * (JT // block) + b
             x = (YS[rows, :].astype(F32) + YR[rows, :].astype(F32)) / count_consumers
             diag = jnp.broadcast_to(ST[0, 1:2, rows], (half, block)).T
-            mine_ids = jnp.broadcast_to(ids[:, rows], (half, block)).T
+            mine_ids = jnp.broadcast_to(ids[:, rows].astype(F32), (half, block)).T
             jac = x - jnp.where(mine_ids == heads, diag, 0.0)
             m = inv[fb]
             out[rows, mine] = jnp.dot(m, jac, precision=lax.Precision.HIGHEST, preferred_element_type=F32)
@@ -457,7 +461,7 @@
 def run_main(n, caug, tastes, coef, colpart, colmean, inverses, ids, cols, sid, asked, count_products, count_consumers):
     LP, LI, W = caug.shape[0], tastes.shape[0], cols.shape[1]
     KA = caug.shape[1]
-    IC, JT = min(512, LI), min(256, LP)
+    IC, JT = min(512, LI), min(512, LP)
     nc, nt = LI // IC, LP // JT
     half = W // 2
     dma = pltpu.SemaphoreType.DMA
@@ -514,7 +518,7 @@
     )
     response, sm = run_main(
         n, cfirm, tastes, price_coef[None, :], colpart, colmean, inverses,
-        firm_map.astype(F32)[None, :], panel_cols.astype(F32)[None, :], sid, asked,
+        firm_map[None, :], panel_cols[None, :], sid, asked,
         count_products, count_consumers,
     )
     return sm[2], sm[1], response

time: 104 us -> 94 us (0.904)
  Pallas kernels: 90.3 us -> 82.8 us
  other arithmetic: 8.29 us -> 5.74 us
    pallas_call x1, Pallas kernels: 63 us -> 56.8 us  [run_main(): pl.pallas_call(functools.partial(main_kernel, n, float(count_products), f...]
    convert_element_type x2 -> x0, other arithmetic: 2.55 us -> none  [the longest x1 1.3 us: body(): firm_map.astype(F32)[None, :]]
    pallas_call x1, Pallas kernels: 27.2 us -> 26 us  [prepare(): pl.pallas_call(functools.partial(prep_kernel, n, LP, cp), out_shape=(jax....]
where the time goes in v4:
time: 94 us; the launch traced here: 93.7 us
  Pallas kernels  82.8 us (88%)
  other arithmetic  5.74 us (6%)
  local copies, waits for them, and re-layouts  4.5 us (5%)
    pallas_call x1, Pallas kernels, run_main(): pl.pallas_call(functools.partial(main_kernel, n, float(count_products), f...  56.8 us
    pallas_call x1, Pallas kernels, prepare(): pl.pallas_call(functools.partial(prep_kernel, n, LP, cp), out_shape=(jax....  26 us
    sort x1, other arithmetic, body(): lax.sort(firm_map).reshape(n, 1, pp)  5.74 us
    unnamed x1, local copies, waits for them, and re-layouts  3.04 us

profile of v4, /device:TPU:0, one launch (start us, length us, event | category | flops | bytes accessed | tf_op | source)
XLA Modules:
  0.0 93.7 jit_solution(9869305488518316967)
XLA Ops:
  0.6 5.7 %sort.14 = (s32[2048]{0:T(1024)}, s32[2048]{0:T(1024)}) sort(s32[2048]{0:T(1024)} %param.12, s32[2048]{0:T(1024)S(1)} %iota.3), dimensions={0}, to_apply=%region_0.0 | sort | flops 22528 | bytes 32768 | tf_op jit(solution)/shard_map/sort | solution.py:514
  6.4 26.0 %shard_map.94 = (bf16[2048,256]{1,0:T(8,128)(2,1)}, f32[32,128]{1,0:T(8,128)}, f32[1,256]{1,0:T(1,128)}, s32[8,1,256]{2,1,0:T(1,128)}) custom-call(s32[8,1,256]{2,1,0:T(1,128)} %bitcast.9, s32[1,2048]{1,0:T(1,128)} %bitcast.7, bf16[2048,128]{1,0:T(8,128)(2,1)} %chars.1, f32[1,2048]{1,0:T(1,128)} %bitcast.12, s32[1,256]{1,0:T(1,128)} %bitcast.15), custom_call_target="tpu_custom_call" | custom-call | tf_op jit(solution)/shard_map/pallas_call | solution.py:192
  32.4 56.8 %shard_map.95 = (f32[2048,256]{1,0:T(8,128)}, f32[3,2048]{1,0:T(4,128)}) custom-call(bf16[2048,256]{1,0:T(8,128)(2,1)} %get-tuple-element.12.C, bf16[4096,128]{1,0:T(8,128)(2,1)} %tastes.1, f32[1,4096]{1,0:T(1,128)} %bitcast.11, f32[32,128]{1,0:T(8,128)} %get-tuple-element.13.colpart, f32[1,256]{1,0:T(1,128)} %get-tuple-element.14.colmean, ...), custom_call_target="tpu_custom_call" | custom-call | tf_op jit(solution)/shard_map/pallas_call | solution.py:468
  89.2 1.5 %fusion = (f32[1,2048]{1,0:T(1,128)}, f32[1,2048]{1,0:T(1,128)}) fusion(f32[3,2048]{1,0:T(4,128)} %get-tuple-element.16), kind=kLoop, calls=%fused_computation | loop fusion | bytes 32768 | tf_op jit(solution)/shard_map/slice | solution.py:524
  90.6 3.0 %copy.11 = f32[2048,256]{1,0:T(8,128)} copy(f32[2048,256]{1,0:T(8,128)} %get-tuple-element.25) | data formatting | bytes 4194304
  (1 shorter events, 0.0 us)
